TPU v7x, 32 devices: a whole 2x2x4 slice. The times are simulated.
32 devices in a mesh: row: 4 (over y, x), col: 4 (over z), tp: 2 (over core).
Axes of the slice: x: 2, y: 2, z: 4, core: 2. Of those that a mesh axis runs over, the one named last changes fastest.
Arguments:
- act_one: bfloat16 [4, 4, 256, 8192], P('row', 'col', None, 'tp'), may hold values from -6 to 6
- residual: bfloat16 [4, 4, 256, 2048], P('row', 'col', None, 'tp'), may hold values from -6 to 6
- upstream: bfloat16 [4, 4, 256, 8192], P('row', 'col', None, 'tp'), may hold values from -6 to 6
- stream_grad: bfloat16 [4, 4, 256, 256], P('row', 'col'), may hold values from -6 to 6
- token_ids: int32 [4, 4, 256], P('row', 'col'), may hold values from 0 to 31999, as said below
- shard_counts: int32 [4, 4], P('row', 'col'), may hold values from 1024 to 21463
- out_one: bfloat16 [4, 8192, 2048], P('col', 'tp', 'row'), may hold values from -6 to 6
- in_two: bfloat16 [4, 8192, 2048], P('row', 'tp', 'col'), may hold values from -6 to 6
- out_one_moment: float32 [4, 8192, 256], P('col', 'tp', 'row'), may hold values from -3 to 3
- in_two_moment: float32 [4, 8192, 256], P('row', 'tp', 'col'), may hold values from -3 to 3
Outputs:
- out_one_new: float32 [4, 8192, 256], P('col', 'tp', 'row')
- out_one_moment_new: float32 [4, 8192, 256], P('col', 'tp', 'row')
- in_two_new: float32 [4, 8192, 256], P('row', 'tp', 'col')
- in_two_moment_new: float32 [4, 8192, 256], P('row', 'tp', 'col')
Inputs may be any that keep to these rules, and one draw needn't show every extreme that they name: `token_ids`: id 0 marks padding and appears only at the end of a path's tokens.
All inputs are finite; a program needn't handle non-finite values.
Results may differ from a plain program's by a relative error of at most 0.017.
Values may be sent and summed in bfloat16 or wider, within the bound.
No kernel may reach another device: no remote copies, remote signals or barrier semaphores. Data moves between devices by JAX's collectives and lax.ppermute only.
A program may use at most 128 MiB of HBM per device.

v0:
```python
import functools
import math

import jax
import jax.numpy as jnp
from jax import lax
from jax.experimental import pallas as pl
from jax.experimental.pallas import tpu as pltpu
from jax.sharding import PartitionSpec as P


inner_rate = 4.0
outer_rate = 0.7
momentum_decay = 0.9


f32 = jnp.float32
bf16 = jnp.bfloat16


def swap(values, axis, step):
    if step == 0:
        return values
    count = lax.axis_size(axis)
    return lax.ppermute(values, axis, [(i, i ^ step) for i in range(count)])


def after(values, *others):
    return lax.optimization_barrier((values,) + others)[0]


def arrange(pieces, key):
    bit = 1
    while bit < len(pieces):
        flip = (key & bit) != 0
        pieces = [jnp.where(flip, pieces[i ^ bit], pieces[i]) for i in range(len(pieces))]
        bit *= 2
    return pieces


def part(values, index, size, dim):
    return lax.dynamic_slice_in_dim(values, index * size, size, dim)


def nt(left, right):
    return lax.dot_general(left, right, (((1,), (1,)), ((), ())), preferred_element_type=f32)


def slope_of(pre, up):
    squash = jax.nn.sigmoid(pre)
    return (up.astype(f32) * squash * (1.0 + pre * (1.0 - squash))).astype(bf16)


def updated(piece, moment, delta):
    moment_new = momentum_decay * moment + delta
    fresh = piece.astype(f32) - outer_rate * (delta + momentum_decay * moment_new)
    return fresh, moment_new


vmem = pl.BlockSpec(memory_space=pltpu.VMEM)
smem = pl.BlockSpec(memory_space=pltpu.SMEM)


def kernel_call(kernel, outs, args, flops=0, scratch=(), exps=0):
    outs = [jax.ShapeDtypeStruct(shape, kind) for shape, kind in outs]
    size = lambda x: math.prod(x.shape) * jnp.dtype(x.dtype).itemsize
    return pl.pallas_call(
        kernel,
        in_specs=[smem if x.size < 16 else vmem for x in args],
        out_specs=[vmem] * len(outs),
        out_shape=outs,
        scratch_shapes=list(scratch),
        compiler_params=pltpu.CompilerParams(vmem_limit_bytes=16 << 20),
        cost_estimate=pl.CostEstimate(
            flops=flops,
            bytes_accessed=sum(size(x) for x in outs) + sum(size(x) for x in args),
            transcendentals=exps,
        ),
    )(*args)


def join_kernel(count, *refs):
    base, arrived, out = refs[:count], refs[count : 2 * count], refs[2 * count]
    sub = base[0].shape[1]
    for j in range(count):
        total = base[j][...].astype(f32) + arrived[j][...].astype(f32)
        out[:, j * sub : (j + 1) * sub] = total.astype(bf16)


def join(base, arrived):
    tok, sub = base[0].shape
    count = len(base)
    outs = [((tok, count * sub), bf16)]
    return kernel_call(functools.partial(join_kernel, count), outs, base + arrived)[0]


def pick_kernel(share, key, *refs):
    pieces, out = refs[:-1], refs[-1]
    for m, piece in enumerate(pieces):
        at = pl.ds(pl.multiple_of((m ^ key[0]) * share, share), share)
        out[at, :] = piece[:, :128].T[:share]


def pick(key, pieces, share):
    outs = [((len(pieces) * share, pieces[0].shape[0]), bf16)]
    return kernel_call(functools.partial(pick_kernel, share), outs, [key] + pieces)[0]


def pre_kernel(scale, share, key, same, other, *refs):
    pieces, (pre, front, stream) = refs[:-3], refs[-3:]
    block = pieces[0].shape[1]
    sub = block // 2
    for m in range(len(pieces)):
        at = pl.ds(pl.multiple_of((m ^ key[0]) * sub, sub), sub)
        mine = m * block + key[1] * sub
        theirs = m * block + (1 - key[1]) * sub
        stream[:, pl.ds(pl.multiple_of(mine, sub), sub)] = same[:, at]
        stream[:, pl.ds(pl.multiple_of(theirs, sub), sub)] = other[:, at]
    for m in range(len(pieces)):
        front[m * share : (m + 1) * share, :] = stream[:, m * block : m * block + 128].T[:share]
    total = nt(pieces[0][...], stream[:, :block])
    for m in range(1, len(pieces)):
        total += nt(pieces[m][...], stream[:, m * block : (m + 1) * block])
    pre[...] = total * scale


def pre_second(key, same, other, pieces, share, scale):
    tok = same.shape[0]
    chunk, block = pieces[0].shape
    count = len(pieces)
    return kernel_call(
        functools.partial(pre_kernel, scale, share),
        [((chunk, tok), f32), ((count * share, tok), bf16)],
        [key, same, other] + pieces,
        flops=2 * tok * chunk * count * block,
        scratch=[pltpu.VMEM((tok, count * block), bf16)],
    )


def slope_kernel(scale, rate, step, groups, pre, up, picked, front, *refs):
    last = groups > 1
    before, carried, seen = refs[: -2 - groups], refs[-2 - groups], refs[-1 - groups]
    totals = refs[-groups:]
    share = totals[0].shape[0]
    chunk = pre.shape[0]
    digits = up[chunk : chunk + 16, :].astype(f32)
    number = digits[0:1] + 256.0 * digits[1:2] + 65536.0 * digits[2:3]
    seen[...] = number + before[0][...] if before else number
    weight = number * rate
    if last:
        norm = 1.0 / seen[...]
    sums = None
    for start in range(0, chunk, step):
        rows = slice(start, start + step)
        slope = slope_of(pre[rows, :], up[rows, :])
        add = jnp.dot(picked[:, rows], slope, preferred_element_type=f32)
        sums = add if sums is None else sums + add
        grad = nt(front[...], slope) * weight[:, :step]
        if before:
            grad += before[1][:, rows]
        if last:
            grad = (grad * norm[:, :step]).astype(bf16)
        for m, total in enumerate(totals):
            total[:, rows] = grad[m * share : (m + 1) * share]
    carried[...] = (sums * scale).astype(bf16)


def level_two(pre, up, picked, front, before, scale, rate, groups):
    chunk, tok = pre.shape
    cols = picked.shape[0]
    step = min(math.gcd(chunk, 256), tok)
    return kernel_call(
        functools.partial(slope_kernel, scale, rate, step, groups),
        [((cols, tok), bf16), ((1, tok), f32)]
        + [((cols // groups, chunk), bf16 if groups > 1 else f32)] * groups,
        [pre, up, picked, front] + before,
        flops=4 * tok * cols * chunk,
        exps=tok * chunk,
    )


def add_kernel(*refs):
    total = refs[0][...].astype(f32)
    for ref in refs[1:-1]:
        total += ref[...].astype(f32)
    refs[-1][...] = total.astype(bf16)


def add_up(pieces):
    return kernel_call(add_kernel, [(pieces[0].shape, bf16)], pieces)[0]


def back_kernel(share, mine, theirs, stream, rate, *groups):
    total = stream[...].astype(f32) + mine[...].astype(f32) + theirs[...].astype(f32)
    total = (total * rate[0]).astype(bf16)
    for j, group in enumerate(groups):
        group[...] = total[j * share : (j + 1) * share]


def back_groups(mine, theirs, stream, rate, share):
    cols, tok = stream.shape
    return kernel_call(
        functools.partial(back_kernel, share),
        [((share, tok), bf16)] * (cols // share),
        [mine, theirs, stream, rate],
    )


def outer_kernel(key, piece, moment, *refs):
    deltas, (fresh, moment_new) = refs[:-2], refs[-2:]
    chunk = deltas[0].shape[1]
    for m, delta in enumerate(deltas):
        at = pl.ds(pl.multiple_of((m ^ key[0]) * chunk, chunk), chunk)
        fresh[:, at], moment_new[:, at] = updated(
            piece[:, at], moment[:, at], delta[...].astype(f32)
        )


def outer_chunks(key, piece, moment, deltas):
    outs = [(piece.shape, f32)] * 2
    return kernel_call(outer_kernel, outs, [key, piece, moment] + deltas)


def hold_kernel(*refs):
    out, start = refs[-1], 0
    for piece in refs[:-1]:
        out[start : start + piece.shape[0], :] = piece[...]
        start += piece.shape[0]


def hold(pieces):
    rows = sum(x.shape[0] for x in pieces)
    return kernel_call(hold_kernel, [((rows, pieces[0].shape[1]), bf16)], pieces)[0]


def finish_kernel(step, *refs):
    groups, (acts, piece, moment, fresh, moment_new) = refs[:-5], refs[-5:]
    group = jnp.concatenate([g[...] for g in groups], axis=1)

    @pl.loop(0, piece.shape[1] // step)
    def _(i):
        at = pl.ds(pl.multiple_of(i * step, step), step)
        delta = jnp.dot(group, acts[:, at], preferred_element_type=f32)
        fresh[:, at], moment_new[:, at] = updated(piece[:, at], moment[:, at], delta)


def finish(groups, acts, piece, moment):
    share, hid = piece.shape
    return kernel_call(
        functools.partial(finish_kernel, math.gcd(hid, 1024)),
        [((share, hid), f32)] * 2,
        groups + [acts, piece, moment],
        flops=2 * share * hid * acts.shape[0],
    )


def on_device(
    act_one,
    residual,
    upstream,
    stream_grad,
    token_ids,
    shard_counts,
    out_one,
    in_two,
    out_one_moment,
    in_two_moment,
):
    n_r, n_c, n_t = (lax.axis_size(a) for a in ("row", "col", "tp"))
    r, c, k = (lax.axis_index(a) for a in ("row", "col", "tp"))
    if n_r != n_c or (n_r & (n_r - 1)) or (n_t & (n_t - 1)):
        raise ValueError("mesh")
    act = act_one[0, 0]
    first_store = out_one[0]
    second_store = in_two[0]
    tok, hid = act.shape
    wide = residual.shape[3] * n_t
    cols = stream_grad.shape[3]
    block = wide // n_r
    sub = block // n_t
    chunk = hid // n_c
    share = cols // n_r
    scale_model = 1.0 / math.sqrt(wide)
    scale_hidden = 1.0 / math.sqrt(hid * n_t)
    kernels = n_t == 2 and sub % 128 == 0 and share <= 128 and chunk % 256 == 0

    farthest = sorted(range(1, n_c), reverse=True)
    sent = [part(second_store, c ^ m, chunk, 0) for m in farthest]
    weights = {m: swap(piece, "col", m) for m, piece in zip(farthest, sent)}
    act_out = after(act, *sent)
    mine = after(residual[0, 0], *sent)
    resid_all = [swap(mine, "tp", t) for t in range(n_t)]
    gate = resid_all[-1]
    weights[0] = part(after(second_store, gate), c, chunk, 0)
    acts = {0: [act]}
    for j in sorted(range(1, n_r), key=lambda j: j.bit_count()):
        bits = [1 << b for b in range(n_r.bit_length()) if j >> b & 1]
        if len(bits) == 1:
            acts[j] = [swap(act_out, "row", j)]
        else:
            low, high = bits[0], bits[-1]
            lower = jnp.concatenate(acts[j ^ low])[: tok // 2]
            upper = jnp.concatenate(acts[j ^ high])[tok // 2 :]
            acts[j] = [swap(lower, "row", low), swap(upper, "row", high)]
    keep = (after(token_ids[0, 0], gate) != 0)[:, None]
    up = after(upstream[0, 0], gate)
    up = jnp.where(keep, up, jnp.zeros_like(up)).T
    number = shard_counts[0, 0]
    digits = jnp.stack([(number >> s) & 255 for s in (0, 8, 16)]).astype(bf16)
    digits = jnp.pad(jnp.broadcast_to(digits[:, None], (3, tok)), ((0, 13), (0, 0)))
    sent_ups = [
        jnp.concatenate([part(up, c ^ m, chunk, 0), digits], axis=0) for m in range(n_c)
    ]
    ups = [swap(sent_ups[m], "col", m) for m in range(n_c)]

    resid_all = jnp.stack(resid_all)
    per = wide // n_t
    resid = []
    for j in range(n_r):
        start = (r ^ j) * block + k * sub
        resid.append(
            lax.dynamic_slice(resid_all, ((start // per) ^ k, 0, start % per), (1, tok, sub))[0]
        )

    stream_rows = after(stream_grad[0, 0], gate)
    stream_rows = jnp.where(keep, stream_rows, jnp.zeros_like(stream_rows)).T
    stream_rows = jnp.concatenate(
        arrange([stream_rows[j * share : (j + 1) * share] for j in range(n_r)], r), axis=0
    )
    piece_one = after(first_store, gate)[:, :share].T
    piece_two = after(second_store, gate)[:, :share].T
    ready = [weights[0], stream_rows, piece_one, piece_two] + resid + sent_ups

    mine = []
    for j in range(n_r):
        behind = ready if j else [gate]
        partial_value = [
            jnp.dot(after(a, *behind), first_store, preferred_element_type=f32)
            for a in acts[j]
        ]
        partial_value = jnp.concatenate([(p * scale_hidden).astype(bf16) for p in partial_value])
        if j == 0:
            ready.append(partial_value)
        summed = part(partial_value, k, sub, 1).astype(f32)
        for t in range(1, n_t):
            summed += swap(part(partial_value, k ^ t, sub, 1), "tp", t).astype(f32)
        mine.append(swap(summed.astype(bf16), "row", j))
    if kernels:
        own = join(resid, mine)
    else:
        own = jnp.concatenate([b.astype(f32) + a.astype(f32) for b, a in zip(resid, mine)], axis=1)
        own = own.astype(bf16)

    count = after(shard_counts[0], own)
    weight_row = [swap(count, "row", j).astype(f32) for j in range(n_r)]
    total_one = sum(weight_row)

    halves = {0: own}
    bit = n_c // 2
    while bit:
        for m in list(halves):
            halves[m | bit] = swap(halves[m], "col", bit)
        bit //= 2
    pieces = [weights[m] for m in range(n_c)]
    key = jnp.stack([c ^ r, k]).astype(jnp.int32)
    if kernels:
        picked = pick(key, pieces, share)
    else:
        picked = jnp.concatenate(arrange([p[:, :share].T for p in pieces], c ^ r), axis=0)
        weight = jnp.concatenate(arrange(pieces, c ^ r), axis=1)

    sums = []
    total_two = 0.0
    arrived = []
    for m in range(n_c):
        streams = [swap(halves[m], "tp", t) for t in range(n_t)]
        if kernels:
            pre, front = pre_second(
                key, streams[0], streams[1], pieces, share, scale_model
            )
            carried, *sums = level_two(
                pre,
                ups[m],
                picked,
                front,
                sums,
                scale_model,
                inner_rate * scale_model,
                n_c if m == n_c - 1 else 1,
            )
            grad_two = sums[1:]
        else:
            around = arrange([s.reshape(tok, n_r, sub) for s in streams], k)
            stream = jnp.stack(around, axis=2).reshape(tok, wide)
            slope = slope_of(nt(weight, stream) * scale_model, ups[m][:chunk])
            given = ups[m][chunk : chunk + 3, 0].astype(f32)
            given = given[0] + 256.0 * given[1] + 65536.0 * given[2]
            total_two += given
            carried = jnp.dot(picked, slope, preferred_element_type=f32)
            carried = (carried * scale_model).astype(bf16)
            front = stream.reshape(tok, n_c, block)[:, :, :share]
            front = jnp.stack(arrange([front[:, j] for j in range(n_c)], c ^ r), axis=1)
            grad = nt(front.reshape(tok, cols).T, slope) * (given * (inner_rate * scale_model))
            sums.append(grad)
            grad_two = (sum(sums) / total_two).astype(bf16)
            grad_two = [grad_two[m * share : (m + 1) * share] for m in range(n_c)]
        arrived.append(swap(carried, "col", m))

    rate = weight_row[0] * (inner_rate * scale_hidden) / total_one
    if kernels:
        partial_value = add_up(arrived)
        theirs = swap(partial_value, "tp", 1)
        groups = back_groups(partial_value, theirs, stream_rows, rate, share)
    else:
        partial_value = sum(a.astype(f32) for a in arrived).astype(bf16)
        back = stream_rows.astype(f32)
        for t in range(n_t):
            back += swap(partial_value, "tp", t).astype(f32)
        back = (back * rate).astype(bf16)
        groups = [back[j * share : (j + 1) * share] for j in range(n_r)]
    groups = [swap(groups[j], "row", j) for j in range(n_r)]

    deltas = [swap(grad_two[m], "col", m) for m in range(n_c)]
    moment_one, moment_two = out_one_moment[0].T, in_two_moment[0].T
    if kernels:
        held = hold([a for j in range(n_r) for a in acts[j]])
        own_key = jnp.stack([c, k]).astype(jnp.int32)
        fresh_two = outer_chunks(own_key, piece_two, moment_two, deltas)
        fresh_one = finish(groups, held, piece_one, moment_one)
    else:
        delta_two = jnp.concatenate(arrange(deltas, c), axis=1).astype(f32)
        fresh_two = updated(piece_two, moment_two, delta_two)
        delta_one = sum(
            jnp.dot(groups[j], jnp.concatenate(acts[j]), preferred_element_type=f32)
            for j in range(n_r)
        )
        fresh_one = updated(piece_one, moment_one, delta_one)
    return tuple(x.T[None] for x in tuple(fresh_one) + tuple(fresh_two))


def solution(mesh):
    return jax.shard_map(
        on_device,
        mesh=mesh,
        in_specs=(
            P("row", "col", None, "tp"),
            P("row", "col", None, "tp"),
            P("row", "col", None, "tp"),
            P("row", "col", None, None),
            P("row", "col", None),
            P("row", "col"),
            P("col", "tp", "row"),
            P("row", "tp", "col"),
            P("col", "tp", "row"),
            P("row", "tp", "col"),
        ),
        out_specs=(
            P("col", "tp", "row"),
            P("col", "tp", "row"),
            P("row", "tp", "col"),
            P("row", "tp", "col"),
        ),
        check_vma=False,
    )
```

profile of v0, /device:TPU:0, one launch (start us, length us, event | category | flops | bytes accessed | tf_op | source)
XLA Modules:
  0.0 238.6 jit_solution(13937247363309590016)
XLA Ops:
  0.7 3.6 %dynamic-slice_bitcast_fusion = (bf16[1024,512]{1,0:T(8,128)(2,1)}, bf16[1024,512]{1,0:T(8,128)(2,1)}, bf16[1024,512]{1,0:T(8,128)(2,1)}) fusion(bf16[1,4096,512]{2,1,0:T(8,128)(2,1)} %param.17, s32[]{:T(128)S(6)} %select_n.132, s32[]{:T(128)S(6)} %select_n.131, s32[]{:T(128)S(6)} %select_n.130), kind=kLoop, calls=%fused_computation.29 | loop fusion | bytes 6291468 | tf_op jit(solution)/shard_map/dynamic_slice | solution.py:42
  4.8 2.5 %collective-permute-start.2 = (bf16[256,4096]{1,0:T(8,128)(2,1)}, bf16[256,4096]{1,0:T(8,128)(2,1)}, u32[]{:S(2)}, u32[]{:S(2)}) collective-permute-start(bf16[256,4096]{1,0:T(8,128)(2,1)} %bitcast.12.refs_0_), channel_id=1, source_target_pairs={{0,8},{8,0},{16,24},{24,16},{1,9},{9,1},{17,25},{25,17},{2,10},{10... | collective-permute-start | bytes 6291464 | tf_op jit(solution)/shard_map/ppermute | solution.py:25
  10.4 2.6 %collective-permute-start.14 = (bf16[1024,512]{1,0:T(8,128)(2,1)}, bf16[1024,512]{1,0:T(8,128)(2,1)S(1)}, u32[]{:S(2)}, u32[]{:S(2)}) collective-permute-start(bf16[1024,512]{1,0:T(8,128)(2,1)} %get-tuple-element.91), channel_id=1, source_target_pairs={{0,4},{2,6},{4,0},{6,2},{1,5},{3,7},{5,1},{7,3},{8,12},{10,14},{12... | collective-permute-start | bytes 3145736 | tf_op jit(solution)/shard_map/ppermute | solution.py:25
  13.0 6.5 %copy.15 = bf16[1,4096,512]{1,2,0:T(8,128)(2,1)} copy(bf16[1,4096,512]{2,1,0:T(8,128)(2,1)} %param.17) | data formatting | bytes 8388608 | tf_op args[7]
  19.6 6.4 %copy.14 = bf16[1,4096,512]{1,2,0:T(8,128)(2,1)} copy(bf16[1,4096,512]{2,1,0:T(8,128)(2,1)} %param.16) | data formatting | bytes 8388608 | tf_op args[6]
  26.0 4.1 %copy.17 = bf16[1,1,256,4096]{2,3,1,0:T(8,128)(2,1)} copy(bf16[1,1,256,4096]{3,2,1,0:T(8,128)(2,1)} %param.12) | data formatting | bytes 4194304 | tf_op args[2]
  31.0 4.2 %fusion.25 = bf16[256,512]{1,0:T(8,128)(2,1)S(1)} fusion(bf16[256,4096]{1,0:T(8,128)(2,1)} %bitcast.12.refs_0_, bf16[1,4096,512]{2,1,0:T(8,128)(2,1)} %param.16), kind=kOutput, calls=%fused_computation.24 | convolution fusion | flops 1074003968 | bytes 6553600 | tf_op jit(solution)/shard_map/dot_general | solution.py:338
  37.9 2.3 constant_dynamic-slice_fusion.2
  44.1 9.8 %collective-permute-done.2.refs_1_ = bf16[256,4096]{1,0:T(8,128)(2,1)} collective-permute-done((bf16[256,4096]{1,0:T(8,128)(2,1)}, bf16[256,4096]{1,0:T(8,128)(2,1)}, u32[]{:S(2)}, u32[]{:S(2)}) %collective-permute-start.2) | collective-permute-done | bytes 2097184 | tf_op jit(solution)/shard_map/ppermute | solution.py:25
  57.1 2.9 %fusion.22 = bf16[256,512]{1,0:T(8,128)(2,1)S(1)} fusion(bf16[256,4096]{1,0:T(8,128)(2,1)} %collective-permute-done.2.refs_1_, bf16[1,4096,512]{2,1,0:T(8,128)(2,1)S(1)} %copy-done.18), kind=kOutput, calls=%fused_computation.23 | convolution fusion | flops 1074003968 | bytes 6553600 | tf_op jit(solution)/shard_map/dot_general | solution.py:338
  63.2 2.9 %fusion.19 = bf16[256,512]{1,0:T(8,128)(2,1)S(1)} fusion(bf16[256,4096]{1,0:T(8,128)(2,1)} %collective-permute-done.5.refs_2_, bf16[1,4096,512]{2,1,0:T(8,128)(2,1)S(1)} %copy-done.18), kind=kOutput, calls=%fused_computation.22 | convolution fusion | flops 1074003968 | bytes 6553600 | tf_op jit(solution)/shard_map/dot_general | solution.py:338
  66.1 3.7 %collective-permute-start.15 = (bf16[1024,512]{1,0:T(8,128)(2,1)}, bf16[1024,512]{1,0:T(8,128)(2,1)S(1)}, u32[]{:S(2)}, u32[]{:S(2)}) collective-permute-start(bf16[1024,512]{1,0:T(8,128)(2,1)} %get-tuple-element.92), channel_id=1, source_target_pairs={{0,6},{2,4},{4,2},{6,0},{1,7},{3,5},{5,3},{7,1},{8,14},{10,12},{12... | collective-permute-start | bytes 3145736 | tf_op jit(solution)/shard_map/ppermute | solution.py:25
  69.8 11.4 %collective-permute-done.8.refs_3_ = bf16[128,4096]{1,0:T(8,128)(2,1)S(1)} collective-permute-done((bf16[128,4096]{1,0:T(8,128)(2,1)S(1)}, bf16[128,4096]{1,0:T(8,128)(2,1)S(1)}, u32[]{:S(2)}, u32[]{:S(2)}) %collective-permute-start.8) | collective-permute-done | bytes 1048608 | tf_op jit(solution)/shard_map/ppermute | solution.py:25
  82.2 4.8 %collective-permute-done.9.refs_4_ = bf16[128,4096]{1,0:T(8,128)(2,1)S(1)} collective-permute-done((bf16[128,4096]{1,0:T(8,128)(2,1)S(1)}, bf16[128,4096]{1,0:T(8,128)(2,1)S(1)}, u32[]{:S(2)}, u32[]{:S(2)}) %collective-permute-start.9) | collective-permute-done | bytes 1048608 | tf_op jit(solution)/shard_map/ppermute | solution.py:25
  95.2 2.6 %collective-permute-start.11 = (bf16[256,256]{1,0:T(8,128)(2,1)S(1)}, bf16[256,256]{1,0:T(8,128)(2,1)S(1)}, u32[]{:S(2)}, u32[]{:S(2)}) collective-permute-start(bf16[256,256]{1,0:T(8,128)(2,1)S(1)} %add_convert_fusion), channel_id=1, source_target_pairs={{0,24},{8,16},{16,8},{24,0},{1,25},{9,17},{17,9},{25,1},{2,26},{10... | collective-permute-start | bytes 393224 | tf_op jit(solution)/shard_map/ppermute | solution.py:25
  97.9 3.2 %collective-permute-done.11.refs_7_ = bf16[256,256]{1,0:T(8,128)(2,1)S(1)} collective-permute-done((bf16[256,256]{1,0:T(8,128)(2,1)S(1)}, bf16[256,256]{1,0:T(8,128)(2,1)S(1)}, u32[]{:S(2)}, u32[]{:S(2)}) %collective-permute-start.11) | collective-permute-done | bytes 131104 | tf_op jit(solution)/shard_map/ppermute | solution.py:25
  101.3 2.8 %collective-permute-start.20 = (bf16[256,1024]{1,0:T(8,128)(2,1)S(1)}, bf16[256,1024]{1,0:T(8,128)(2,1)}, u32[]{:S(2)}, u32[]{:S(2)}) collective-permute-start(bf16[256,1024]{1,0:T(8,128)(2,1)S(1)} %shard_map.129.same), channel_id=1, source_target_pairs={{0,4},{2,6},{4,0},{6,2},{1,5},{3,7},{5,1},{7,3},{8,12},{10,14},{12... | collective-permute-start | bytes 1572872 | tf_op jit(solution)/shard_map/ppermute | solution.py:25
  106.5 31.2 %collective-permute-done.20.same = bf16[256,1024]{1,0:T(8,128)(2,1)} collective-permute-done((bf16[256,1024]{1,0:T(8,128)(2,1)S(1)}, bf16[256,1024]{1,0:T(8,128)(2,1)}, u32[]{:S(2)}, u32[]{:S(2)}) %collective-permute-start.20) | collective-permute-done | bytes 524320 | tf_op jit(solution)/shard_map/ppermute | solution.py:25
  143.9 20.4 %collective-permute-done.24.same = bf16[256,1024]{1,0:T(8,128)(2,1)} collective-permute-done((bf16[256,1024]{1,0:T(8,128)(2,1)}, bf16[256,1024]{1,0:T(8,128)(2,1)}, u32[]{:S(2)}, u32[]{:S(2)}) %collective-permute-start.24) | collective-permute-done | bytes 524320 | tf_op jit(solution)/shard_map/ppermute | solution.py:25
  164.2 2.5 %collective-permute-start.26 = (bf16[1040,256]{1,0:T(8,128)(2,1)}, bf16[1040,256]{1,0:T(8,128)(2,1)}, u32[]{:S(2)}, u32[]{:S(2)}) collective-permute-start(bf16[1040,256]{1,0:T(8,128)(2,1)} %get-tuple-element.105), channel_id=1, source_target_pairs={{0,6},{2,4},{4,2},{6,0},{1,7},{3,5},{5,3},{7,1},{8,14},{10,12},{12... | collective-permute-start | bytes 1597448 | tf_op jit(solution)/shard_map/ppermute | solution.py:25
  174.2 2.5 %shard_map.133 = (f32[1024,256]{1,0:T(8,128)S(1)}, bf16[256,256]{1,0:T(8,128)(2,1)S(1)}) custom-call(s32[2]{0:T(128)S(1)} %pad_add_fusion.key, bf16[256,1024]{1,0:T(8,128)(2,1)S(1)} %copy-done.15, bf16[256,1024]{1,0:T(8,128)(2,1)} %collective-permute-done.17.other, bf16[1024,512]{1,0:T(8,128)(2,1)S(1)} %copy.18.refs_0_, ...), custom_call_target="tpu_custom_call" | custom-call | flops 1073741824 | bytes 6422536 | tf_op jit(solution)/shard_map/pallas_call | solution.py:67
  178.5 2.7 %shard_map.135 = (f32[1024,256]{1,0:T(8,128)S(1)}, bf16[256,256]{1,0:T(8,128)(2,1)S(1)}) custom-call(s32[2]{0:T(128)S(1)} %pad_add_fusion.key, bf16[256,1024]{1,0:T(8,128)(2,1)} %collective-permute-done.20.same, bf16[256,1024]{1,0:T(8,128)(2,1)} %collective-permute-done.21.other, bf16[1024,512]{1,0:T(8,128)(2,1)S(1)} %copy.18.refs_0_, ...), custom_call_target="tpu_custom_call" | custom-call | flops 1073741824 | bytes 6422536 | tf_op jit(solution)/shard_map/pallas_call | solution.py:67
  182.8 11.1 %collective-permute-start.23 = (bf16[256,256]{1,0:T(8,128)(2,1)S(1)}, bf16[256,256]{1,0:T(8,128)(2,1)S(1)}, u32[]{:S(2)}, u32[]{:S(2)}) collective-permute-start(bf16[256,256]{1,0:T(8,128)(2,1)S(1)} %get-tuple-element.71), channel_id=1, source_target_pairs={{0,4},{2,6},{4,0},{6,2},{1,5},{3,7},{5,1},{7,3},{8,12},{10,14},{12... | collective-permute-start | bytes 393224 | tf_op jit(solution)/shard_map/ppermute | solution.py:25
  193.9 2.6 %shard_map.137 = (f32[1024,256]{1,0:T(8,128)S(1)}, bf16[256,256]{1,0:T(8,128)(2,1)S(1)}) custom-call(s32[2]{0:T(128)S(1)} %pad_add_fusion.key, bf16[256,1024]{1,0:T(8,128)(2,1)} %collective-permute-done.24.same, bf16[256,1024]{1,0:T(8,128)(2,1)} %collective-permute-done.25.other, bf16[1024,512]{1,0:T(8,128)(2,1)S(1)} %copy.18.refs_0_, ...), custom_call_target="tpu_custom_call" | custom-call | flops 1073741824 | bytes 6422536 | tf_op jit(solution)/shard_map/pallas_call | solution.py:67
  198.8 7.1 %collective-permute-done.23.refs_2_ = bf16[256,256]{1,0:T(8,128)(2,1)S(1)} collective-permute-done((bf16[256,256]{1,0:T(8,128)(2,1)S(1)}, bf16[256,256]{1,0:T(8,128)(2,1)S(1)}, u32[]{:S(2)}, u32[]{:S(2)}) %collective-permute-start.23) | collective-permute-done | bytes 131104 | tf_op jit(solution)/shard_map/ppermute | solution.py:25
  206.1 4.2 %collective-permute-start.35 = (bf16[64,1024]{1,0:T(8,128)(2,1)S(1)}, bf16[64,1024]{1,0:T(8,128)(2,1)S(1)}, u32[]{:S(2)}, u32[]{:S(2)}) collective-permute-start(bf16[64,1024]{1,0:T(8,128)(2,1)S(1)} %get-tuple-element.85), channel_id=1, source_target_pairs={{0,2},{2,0},{4,6},{6,4},{1,3},{3,1},{5,7},{7,5},{8,10},{10,8},{12,... | collective-permute-start | bytes 393224 | tf_op jit(solution)/shard_map/ppermute | solution.py:25
  210.3 2.4 %collective-permute-start.37 = (bf16[64,1024]{1,0:T(8,128)(2,1)S(1)}, bf16[64,1024]{1,0:T(8,128)(2,1)S(1)}, u32[]{:S(2)}, u32[]{:S(2)}) collective-permute-start(bf16[64,1024]{1,0:T(8,128)(2,1)S(1)} %get-tuple-element.87), channel_id=1, source_target_pairs={{0,6},{2,4},{4,2},{6,0},{1,7},{3,5},{5,3},{7,1},{8,14},{10,12},{12... | collective-permute-start | bytes 393224 | tf_op jit(solution)/shard_map/ppermute | solution.py:25
  214.2 2.3 collective-permute-done.29
  217.6 2.7 %collective-permute-done.30 = s32[1]{0:T(128)} collective-permute-done((s32[1]{0:T(128)}, s32[1]{0:T(128)}, u32[]{:S(2)}, u32[]{:S(2)}) %collective-permute-start.30) | collective-permute-done | bytes 36 | tf_op jit(solution)/shard_map/ppermute | solution.py:25
  222.4 2.6 %collective-permute-done.31 = s32[1]{0:T(128)} collective-permute-done((s32[1]{0:T(128)}, s32[1]{0:T(128)}, u32[]{:S(2)}, u32[]{:S(2)}) %collective-permute-start.31) | collective-permute-done | bytes 36 | tf_op jit(solution)/shard_map/ppermute | solution.py:25
  229.4 3.5 %shard_map.141.refs_4_ = bf16[1024,4096]{1,0:T(8,128)(2,1)S(1)} custom-call(bf16[256,4096]{1,0:T(8,128)(2,1)} %bitcast.12.refs_0_, bf16[256,4096]{1,0:T(8,128)(2,1)} %collective-permute-done.2.refs_1_, bf16[256,4096]{1,0:T(8,128)(2,1)} %collective-permute-done.5.refs_2_, bf16[128,4096]{1,0:T(8,128)(2,1)S(1)} %copy-done.4, bf16[128,4096]{1,0:T(8,128)(2,1)S(1)} %copy-done.6), custom_call_target="tpu_custom_call" | custom-call | bytes 16777216 | tf_op jit(solution)/shard_map/pallas_call | solution.py:67
  235.2 3.4 %shard_map.142 = (f32[64,4096]{1,0:T(8,128)}, f32[64,4096]{1,0:T(8,128)}) custom-call(bf16[64,256]{1,0:T(8,128)(2,1)S(1)} %get-tuple-element.78.refs_0_, bf16[64,256]{1,0:T(8,128)(2,1)S(1)} %collective-permute-done.32.refs_1_, bf16[64,256]{1,0:T(8,128)(2,1)S(1)} %collective-permute-done.33.refs_2_, bf16[64,256]{1,0:T(8,128)(2,1)S(1)} %collective-permute-done.34.refs_3_, ...), custom_call_target="tpu_custom_call" | custom-call | flops 536870912 | bytes 12189696 | tf_op jit(solution)/shard_map/pallas_call | solution.py:67
  (141 shorter events, 57.3 us)
Async XLA Ops:
  4.3 26.6 %collective-permute-start = (bf16[256,1024]{1,0:T(8,128)(2,1)S(1)}, bf16[256,1024]{1,0:T(8,128)(2,1)S(1)}, u32[]{:S(2)}, u32[]{:S(2)}) collective-permute-start(bf16[256,1024]{1,0:T(8,128)(2,1)S(1)} %bitcast.109), channel_id=1, source_target_pairs={{0,1},{1,0},{2,3},{3,2},{4,5},{5,4},{6,7},{7,6},{8,9},{9,8},{10,11... | collective-permute-start | bytes 1572872 | tf_op jit(solution)/shard_map/ppermute | solution.py:25
  4.8 49.1 %collective-permute-start.2 = (bf16[256,4096]{1,0:T(8,128)(2,1)}, bf16[256,4096]{1,0:T(8,128)(2,1)}, u32[]{:S(2)}, u32[]{:S(2)}) collective-permute-start(bf16[256,4096]{1,0:T(8,128)(2,1)} %bitcast.12.refs_0_), channel_id=1, source_target_pairs={{0,8},{8,0},{16,24},{24,16},{1,9},{9,1},{17,25},{25,17},{2,10},{10... | collective-permute-start | bytes 6291464 | tf_op jit(solution)/shard_map/ppermute | solution.py:25
  7.3 48.1 %collective-permute-start.5 = (bf16[256,4096]{1,0:T(8,128)(2,1)}, bf16[256,4096]{1,0:T(8,128)(2,1)}, u32[]{:S(2)}, u32[]{:S(2)}) collective-permute-start(bf16[256,4096]{1,0:T(8,128)(2,1)} %bitcast.12.refs_0_), channel_id=1, source_target_pairs={{0,16},{8,24},{16,0},{24,8},{1,17},{9,25},{17,1},{25,9},{2,18},{10... | collective-permute-start | bytes 6291464 | tf_op jit(solution)/shard_map/ppermute | solution.py:25
  8.8 96.9 %collective-permute-start.13 = (bf16[1024,512]{1,0:T(8,128)(2,1)}, bf16[1024,512]{1,0:T(8,128)(2,1)S(1)}, u32[]{:S(2)}, u32[]{:S(2)}) collective-permute-start(bf16[1024,512]{1,0:T(8,128)(2,1)} %get-tuple-element.90), channel_id=1, source_target_pairs={{0,2},{2,0},{4,6},{6,4},{1,3},{3,1},{5,7},{7,5},{8,10},{10,8},{12,... | collective-permute-start | bytes 3145736 | tf_op jit(solution)/shard_map/ppermute | solution.py:25
  10.4 128.2 %collective-permute-start.14 = (bf16[1024,512]{1,0:T(8,128)(2,1)}, bf16[1024,512]{1,0:T(8,128)(2,1)S(1)}, u32[]{:S(2)}, u32[]{:S(2)}) collective-permute-start(bf16[1024,512]{1,0:T(8,128)(2,1)} %get-tuple-element.91), channel_id=1, source_target_pairs={{0,4},{2,6},{4,0},{6,2},{1,5},{3,7},{5,1},{7,3},{8,12},{10,14},{12... | collective-permute-start | bytes 3145736 | tf_op jit(solution)/shard_map/ppermute | solution.py:25
  56.7 24.5 %collective-permute-start.8 = (bf16[128,4096]{1,0:T(8,128)(2,1)S(1)}, bf16[128,4096]{1,0:T(8,128)(2,1)S(1)}, u32[]{:S(2)}, u32[]{:S(2)}) collective-permute-start(bf16[128,4096]{1,0:T(8,128)(2,1)S(1)} %slice.36), channel_id=1, source_target_pairs={{0,8},{8,0},{16,24},{24,16},{1,9},{9,1},{17,25},{25,17},{2,10},{10... | collective-permute-start | bytes 3145736 | tf_op jit(solution)/shard_map/ppermute | solution.py:25
  60.0 6.1 %collective-permute-start.3 = (bf16[256,256]{1,0:T(8,128)(2,1)S(1)}, bf16[256,256]{1,0:T(8,128)(2,1)S(1)}, u32[]{:S(2)}, u32[]{:S(2)}) collective-permute-start(bf16[256,256]{1,0:T(8,128)(2,1)S(1)} %constant_dynamic-slice_fusion.1), channel_id=1, source_target_pairs={{0,1},{1,0},{2,3},{3,2},{4,5},{5,4},{6,7},{7,6},{8,9},{9,8},{10,11... | collective-permute-start | bytes 393224 | tf_op jit(solution)/shard_map/ppermute | solution.py:25
  61.4 25.6 %collective-permute-start.9 = (bf16[128,4096]{1,0:T(8,128)(2,1)S(1)}, bf16[128,4096]{1,0:T(8,128)(2,1)S(1)}, u32[]{:S(2)}, u32[]{:S(2)}) collective-permute-start(bf16[128,4096]{1,0:T(8,128)(2,1)S(1)} %slice.37), channel_id=1, source_target_pairs={{0,16},{8,24},{16,0},{24,8},{1,17},{9,25},{17,1},{25,9},{2,18},{10... | collective-permute-start | bytes 3145736 | tf_op jit(solution)/shard_map/ppermute | solution.py:25
  66.1 74.5 %collective-permute-start.15 = (bf16[1024,512]{1,0:T(8,128)(2,1)}, bf16[1024,512]{1,0:T(8,128)(2,1)S(1)}, u32[]{:S(2)}, u32[]{:S(2)}) collective-permute-start(bf16[1024,512]{1,0:T(8,128)(2,1)} %get-tuple-element.92), channel_id=1, source_target_pairs={{0,6},{2,4},{4,2},{6,0},{1,7},{3,5},{5,3},{7,1},{8,14},{10,12},{12... | collective-permute-start | bytes 3145736 | tf_op jit(solution)/shard_map/ppermute | solution.py:25
  81.2 10.3 %collective-permute-start.1 = (bf16[256,256]{1,0:T(8,128)(2,1)S(1)}, bf16[256,256]{1,0:T(8,128)(2,1)S(1)}, u32[]{:S(2)}, u32[]{:S(2)}) collective-permute-start(bf16[256,256]{1,0:T(8,128)(2,1)S(1)} %constant_dynamic-slice_fusion.3), channel_id=1, source_target_pairs={{0,1},{1,0},{2,3},{3,2},{4,5},{5,4},{6,7},{7,6},{8,9},{9,8},{10,11... | collective-permute-start | bytes 393224 | tf_op jit(solution)/shard_map/ppermute | solution.py:25
  91.4 6.5 %collective-permute-start.7 = (bf16[256,256]{1,0:T(8,128)(2,1)S(1)}, bf16[256,256]{1,0:T(8,128)(2,1)S(1)}, u32[]{:S(2)}, u32[]{:S(2)}) collective-permute-start(bf16[256,256]{1,0:T(8,128)(2,1)S(1)} %add_convert_fusion.1), channel_id=1, source_target_pairs={{0,16},{8,24},{16,0},{24,8},{1,17},{9,25},{17,1},{25,9},{2,18},{10... | collective-permute-start | bytes 393224 | tf_op jit(solution)/shard_map/ppermute | solution.py:25
  95.2 5.9 %collective-permute-start.11 = (bf16[256,256]{1,0:T(8,128)(2,1)S(1)}, bf16[256,256]{1,0:T(8,128)(2,1)S(1)}, u32[]{:S(2)}, u32[]{:S(2)}) collective-permute-start(bf16[256,256]{1,0:T(8,128)(2,1)S(1)} %add_convert_fusion), channel_id=1, source_target_pairs={{0,24},{8,16},{16,8},{24,0},{1,25},{9,17},{17,9},{25,1},{2,26},{10... | collective-permute-start | bytes 393224 | tf_op jit(solution)/shard_map/ppermute | solution.py:25
  101.3 36.4 %collective-permute-start.20 = (bf16[256,1024]{1,0:T(8,128)(2,1)S(1)}, bf16[256,1024]{1,0:T(8,128)(2,1)}, u32[]{:S(2)}, u32[]{:S(2)}) collective-permute-start(bf16[256,1024]{1,0:T(8,128)(2,1)S(1)} %shard_map.129.same), channel_id=1, source_target_pairs={{0,4},{2,6},{4,0},{6,2},{1,5},{3,7},{5,1},{7,3},{8,12},{10,14},{12... | collective-permute-start | bytes 1572872 | tf_op jit(solution)/shard_map/ppermute | solution.py:25
  104.1 33.6 %collective-permute-start.16 = (bf16[256,1024]{1,0:T(8,128)(2,1)S(1)}, bf16[256,1024]{1,0:T(8,128)(2,1)S(1)}, u32[]{:S(2)}, u32[]{:S(2)}) collective-permute-start(bf16[256,1024]{1,0:T(8,128)(2,1)S(1)} %shard_map.129.same), channel_id=1, source_target_pairs={{0,2},{2,0},{4,6},{6,4},{1,3},{3,1},{5,7},{7,5},{8,10},{10,8},{12,... | collective-permute-start | bytes 1572872 | tf_op jit(solution)/shard_map/ppermute | solution.py:25
  105.7 36.1 %collective-permute-start.12 = (bf16[256,1024]{1,0:T(8,128)(2,1)S(1)}, bf16[256,1024]{1,0:T(8,128)(2,1)S(1)}, u32[]{:S(2)}, u32[]{:S(2)}) collective-permute-start(bf16[256,1024]{1,0:T(8,128)(2,1)S(1)} %shard_map.129.same), channel_id=1, source_target_pairs={{0,1},{1,0},{2,3},{3,2},{4,5},{5,4},{6,7},{7,6},{8,9},{9,8},{10,11... | collective-permute-start | bytes 1572872 | tf_op jit(solution)/shard_map/ppermute | solution.py:25
  137.7 26.5 %collective-permute-start.24 = (bf16[256,1024]{1,0:T(8,128)(2,1)}, bf16[256,1024]{1,0:T(8,128)(2,1)}, u32[]{:S(2)}, u32[]{:S(2)}) collective-permute-start(bf16[256,1024]{1,0:T(8,128)(2,1)} %collective-permute-done.20.same), channel_id=1, source_target_pairs={{0,2},{2,0},{4,6},{6,4},{1,3},{3,1},{5,7},{7,5},{8,10},{10,8},{12,... | collective-permute-start | bytes 1572872 | tf_op jit(solution)/shard_map/ppermute | solution.py:25
  137.7 26.5 %collective-permute-start.17 = (bf16[256,1024]{1,0:T(8,128)(2,1)S(1)}, bf16[256,1024]{1,0:T(8,128)(2,1)}, u32[]{:S(2)}, u32[]{:S(2)}) collective-permute-start(bf16[256,1024]{1,0:T(8,128)(2,1)S(1)} %collective-permute-done.16.same), channel_id=1, source_target_pairs={{0,1},{1,0},{2,3},{3,2},{4,5},{5,4},{6,7},{7,6},{8,9},{9,8},{10,11... | collective-permute-start | bytes 1572872 | tf_op jit(solution)/shard_map/ppermute | solution.py:25
  138.6 38.2 %collective-permute-start.18 = (bf16[1040,256]{1,0:T(8,128)(2,1)}, bf16[1040,256]{1,0:T(8,128)(2,1)}, u32[]{:S(2)}, u32[]{:S(2)}) collective-permute-start(bf16[1040,256]{1,0:T(8,128)(2,1)} %get-tuple-element.106), channel_id=1, source_target_pairs={{0,2},{2,0},{4,6},{6,4},{1,3},{3,1},{5,7},{7,5},{8,10},{10,8},{12,... | collective-permute-start | bytes 1597448 | tf_op jit(solution)/shard_map/ppermute | solution.py:25
  141.5 36.9 %collective-permute-start.21 = (bf16[256,1024]{1,0:T(8,128)(2,1)}, bf16[256,1024]{1,0:T(8,128)(2,1)}, u32[]{:S(2)}, u32[]{:S(2)}) collective-permute-start(bf16[256,1024]{1,0:T(8,128)(2,1)} %collective-permute-done.20.same), channel_id=1, source_target_pairs={{0,1},{1,0},{2,3},{3,2},{4,5},{5,4},{6,7},{7,6},{8,9},{9,8},{10,11... | collective-permute-start | bytes 1572872 | tf_op jit(solution)/shard_map/ppermute | solution.py:25
  142.6 38.6 %collective-permute-start.22 = (bf16[1040,256]{1,0:T(8,128)(2,1)}, bf16[1040,256]{1,0:T(8,128)(2,1)}, u32[]{:S(2)}, u32[]{:S(2)}) collective-permute-start(bf16[1040,256]{1,0:T(8,128)(2,1)} %get-tuple-element.107), channel_id=1, source_target_pairs={{0,4},{2,6},{4,0},{6,2},{1,5},{3,7},{5,1},{7,3},{8,12},{10,14},{12... | collective-permute-start | bytes 1597448 | tf_op jit(solution)/shard_map/ppermute | solution.py:25
  164.2 29.7 %collective-permute-start.25 = (bf16[256,1024]{1,0:T(8,128)(2,1)}, bf16[256,1024]{1,0:T(8,128)(2,1)}, u32[]{:S(2)}, u32[]{:S(2)}) collective-permute-start(bf16[256,1024]{1,0:T(8,128)(2,1)} %collective-permute-done.24.same), channel_id=1, source_target_pairs={{0,1},{1,0},{2,3},{3,2},{4,5},{5,4},{6,7},{7,6},{8,9},{9,8},{10,11... | collective-permute-start | bytes 1572872 | tf_op jit(solution)/shard_map/ppermute | solution.py:25
  164.2 32.3 %collective-permute-start.26 = (bf16[1040,256]{1,0:T(8,128)(2,1)}, bf16[1040,256]{1,0:T(8,128)(2,1)}, u32[]{:S(2)}, u32[]{:S(2)}) collective-permute-start(bf16[1040,256]{1,0:T(8,128)(2,1)} %get-tuple-element.105), channel_id=1, source_target_pairs={{0,6},{2,4},{4,2},{6,0},{1,7},{3,5},{5,3},{7,1},{8,14},{10,12},{12... | collective-permute-start | bytes 1597448 | tf_op jit(solution)/shard_map/ppermute | solution.py:25
  178.4 20.4 %collective-permute-start.19 = (bf16[256,256]{1,0:T(8,128)(2,1)S(1)}, bf16[256,256]{1,0:T(8,128)(2,1)S(1)}, u32[]{:S(2)}, u32[]{:S(2)}) collective-permute-start(bf16[256,256]{1,0:T(8,128)(2,1)S(1)} %get-tuple-element.66), channel_id=1, source_target_pairs={{0,2},{2,0},{4,6},{6,4},{1,3},{3,1},{5,7},{7,5},{8,10},{10,8},{12,... | collective-permute-start | bytes 393224 | tf_op jit(solution)/shard_map/ppermute | solution.py:25
  182.8 23.1 %collective-permute-start.23 = (bf16[256,256]{1,0:T(8,128)(2,1)S(1)}, bf16[256,256]{1,0:T(8,128)(2,1)S(1)}, u32[]{:S(2)}, u32[]{:S(2)}) collective-permute-start(bf16[256,256]{1,0:T(8,128)(2,1)S(1)} %get-tuple-element.71), channel_id=1, source_target_pairs={{0,4},{2,6},{4,0},{6,2},{1,5},{3,7},{5,1},{7,3},{8,12},{10,14},{12... | collective-permute-start | bytes 393224 | tf_op jit(solution)/shard_map/ppermute | solution.py:25
  198.8 7.1 %collective-permute-start.27 = (bf16[256,256]{1,0:T(8,128)(2,1)S(1)}, bf16[256,256]{1,0:T(8,128)(2,1)S(1)}, u32[]{:S(2)}, u32[]{:S(2)}) collective-permute-start(bf16[256,256]{1,0:T(8,128)(2,1)S(1)} %get-tuple-element.76), channel_id=1, source_target_pairs={{0,6},{2,4},{4,2},{6,0},{1,7},{3,5},{5,3},{7,1},{8,14},{10,12},{12... | collective-permute-start | bytes 393224 | tf_op jit(solution)/shard_map/ppermute | solution.py:25
  206.0 19.7 %collective-permute-start.28 = (bf16[256,256]{1,0:T(8,128)(2,1)S(1)}, bf16[256,256]{1,0:T(8,128)(2,1)S(1)}, u32[]{:S(2)}, u32[]{:S(2)}) collective-permute-start(bf16[256,256]{1,0:T(8,128)(2,1)S(1)} %shard_map.139.mine), channel_id=1, source_target_pairs={{0,1},{1,0},{2,3},{3,2},{4,5},{5,4},{6,7},{7,6},{8,9},{9,8},{10,11... | collective-permute-start | bytes 393224 | tf_op jit(solution)/shard_map/ppermute | solution.py:25
  206.1 21.7 %collective-permute-start.35 = (bf16[64,1024]{1,0:T(8,128)(2,1)S(1)}, bf16[64,1024]{1,0:T(8,128)(2,1)S(1)}, u32[]{:S(2)}, u32[]{:S(2)}) collective-permute-start(bf16[64,1024]{1,0:T(8,128)(2,1)S(1)} %get-tuple-element.85), channel_id=1, source_target_pairs={{0,2},{2,0},{4,6},{6,4},{1,3},{3,1},{5,7},{7,5},{8,10},{10,8},{12,... | collective-permute-start | bytes 393224 | tf_op jit(solution)/shard_map/ppermute | solution.py:25
  210.3 22.7 %collective-permute-start.36 = (bf16[64,1024]{1,0:T(8,128)(2,1)S(1)}, bf16[64,1024]{1,0:T(8,128)(2,1)S(1)}, u32[]{:S(2)}, u32[]{:S(2)}) collective-permute-start(bf16[64,1024]{1,0:T(8,128)(2,1)S(1)} %get-tuple-element.86), channel_id=1, source_target_pairs={{0,4},{2,6},{4,0},{6,2},{1,5},{3,7},{5,1},{7,3},{8,12},{10,14},{12... | collective-permute-start | bytes 393224 | tf_op jit(solution)/shard_map/ppermute | solution.py:25
  210.3 22.7 %collective-permute-start.37 = (bf16[64,1024]{1,0:T(8,128)(2,1)S(1)}, bf16[64,1024]{1,0:T(8,128)(2,1)S(1)}, u32[]{:S(2)}, u32[]{:S(2)}) collective-permute-start(bf16[64,1024]{1,0:T(8,128)(2,1)S(1)} %get-tuple-element.87), channel_id=1, source_target_pairs={{0,6},{2,4},{4,2},{6,0},{1,7},{3,5},{5,3},{7,1},{8,14},{10,12},{12... | collective-permute-start | bytes 393224 | tf_op jit(solution)/shard_map/ppermute | solution.py:25
  225.8 9.4 %collective-permute-start.32 = (bf16[64,256]{1,0:T(8,128)(2,1)S(1)}, bf16[64,256]{1,0:T(8,128)(2,1)S(1)}, u32[]{:S(2)}, u32[]{:S(2)}) collective-permute-start(bf16[64,256]{1,0:T(8,128)(2,1)S(1)} %get-tuple-element.79), channel_id=1, source_target_pairs={{0,8},{8,0},{16,24},{24,16},{1,9},{9,1},{17,25},{25,17},{2,10},{10... | collective-permute-start | bytes 98312 | tf_op jit(solution)/shard_map/ppermute | solution.py:25
  227.3 7.8 %collective-permute-start.33 = (bf16[64,256]{1,0:T(8,128)(2,1)S(1)}, bf16[64,256]{1,0:T(8,128)(2,1)S(1)}, u32[]{:S(2)}, u32[]{:S(2)}) collective-permute-start(bf16[64,256]{1,0:T(8,128)(2,1)S(1)} %get-tuple-element.80), channel_id=1, source_target_pairs={{0,16},{8,24},{16,0},{24,8},{1,17},{9,25},{17,1},{25,9},{2,18},{10... | collective-permute-start | bytes 98312 | tf_op jit(solution)/shard_map/ppermute | solution.py:25
  227.8 7.3 %collective-permute-start.34 = (bf16[64,256]{1,0:T(8,128)(2,1)S(1)}, bf16[64,256]{1,0:T(8,128)(2,1)S(1)}, u32[]{:S(2)}, u32[]{:S(2)}) collective-permute-start(bf16[64,256]{1,0:T(8,128)(2,1)S(1)} %get-tuple-element.81), channel_id=1, source_target_pairs={{0,24},{8,16},{16,8},{24,0},{1,25},{9,17},{17,9},{25,1},{2,26},{10... | collective-permute-start | bytes 98312 | tf_op jit(solution)/shard_map/ppermute | solution.py:25
  (29 other events, 147.2 us)
where the time goes:
time: 240 us; the launch traced here: 239 us
  waiting for transfers between devices  101 us (42%)
  starting transfers between devices  56 us (23%)
  local copies, waits for them, and re-layouts  37.8 us (16%)
  Pallas kernels  26 us (11%)
  matrix products  11.4 us (5%)
  between operations  3.84 us (2%)
  other arithmetic  2.89 us (1%)
    ppermute x38, waiting for transfers between devices, swap(): return lax.ppermute(values, axis, [(i, i ^ step) for i in range(count)])  101 us
    ppermute x38, starting transfers between devices, swap(): return lax.ppermute(values, axis, [(i, i ^ step) for i in range(count)])  56 us
    pallas_call x15, Pallas kernels, kernel_call(): pl.pallas_call(kernel, in_specs=[smem if x.size < 16 else vmem for x in a...  26 us
    unnamed x50, local copies, waits for them, and re-layouts  23.4 us
    dot_general x5, matrix products, on_device(): jnp.dot(after(a, *behind), first_store, preferred_element_type=f32)  11.4 us
    dynamic_slice x7, local copies, waits for them, and re-layouts, part(): return lax.dynamic_slice_in_dim(values, index * size, size, dim)  7.8 us
  transfers between devices with their start and end apart: 38, of which 14 were waited for; matrix products, arithmetic and copies ran while one was open for 18% of the time, Pallas kernels for 9%

commit v1 on v0

--- a/solution.py
+++ b/solution.py
@@ -61,13 +61,13 @@
 smem = pl.BlockSpec(memory_space=pltpu.SMEM)
 
 
-def kernel_call(kernel, outs, args, flops=0, scratch=(), exps=0):
+def kernel_call(kernel, outs, args, flops=0, scratch=(), exps=0, outs_in=pltpu.VMEM):
     outs = [jax.ShapeDtypeStruct(shape, kind) for shape, kind in outs]
     size = lambda x: math.prod(x.shape) * jnp.dtype(x.dtype).itemsize
     return pl.pallas_call(
         kernel,
         in_specs=[smem if x.size < 16 else vmem for x in args],
-        out_specs=[vmem] * len(outs),
+        out_specs=[pl.BlockSpec(memory_space=outs_in)] * len(outs),
         out_shape=outs,
         scratch_shapes=list(scratch),
         compiler_params=pltpu.CompilerParams(vmem_limit_bytes=16 << 20),
@@ -104,6 +104,23 @@
 def pick(key, pieces, share):
     outs = [((len(pieces) * share, pieces[0].shape[0]), bf16)]
     return kernel_call(functools.partial(pick_kernel, share), outs, [key] + pieces)[0]
+
+
+def lead_kernel(share, store, out):
+    out[...] = store[...].T[:share]
+
+
+def lead(store, share):
+    hid = store.shape[0]
+    step = math.gcd(hid, 512)
+    return pl.pallas_call(
+        functools.partial(lead_kernel, share),
+        grid=(hid // step,),
+        in_specs=[pl.BlockSpec((step, 128), lambda i: (i, 0))],
+        out_specs=pl.BlockSpec((share, step), lambda i: (0, i)),
+        out_shape=jax.ShapeDtypeStruct((share, hid), bf16),
+        name="lead",
+    )(store)
 
 
 def pre_kernel(scale, share, key, same, other, *refs):
@@ -137,11 +154,13 @@
     )
 
 
-def slope_kernel(scale, rate, step, groups, pre, up, picked, front, *refs):
+def slope_kernel(scale, rate, step, groups, key, pre, up, picked, front, *refs):
     last = groups > 1
-    before, carried, seen = refs[: -2 - groups], refs[-2 - groups], refs[-1 - groups]
+    refs, scratch = refs[:-1], refs[-1]
     totals = refs[-groups:]
     share = totals[0].shape[0]
+    seen, refs = refs[-1 - groups], refs[: -1 - groups]
+    before, carried = (refs[:-1], refs[-1:]) if last else (refs[:-2], refs[-2:])
     chunk = pre.shape[0]
     digits = up[chunk : chunk + 16, :].astype(f32)
     number = digits[0:1] + 256.0 * digits[1:2] + 65536.0 * digits[2:3]
@@ -162,19 +181,27 @@
             grad = (grad * norm[:, :step]).astype(bf16)
         for m, total in enumerate(totals):
             total[:, rows] = grad[m * share : (m + 1) * share]
-    carried[...] = (sums * scale).astype(bf16)
-
-
-def level_two(pre, up, picked, front, before, scale, rate, groups):
+    if last:
+        carried[0][...] = (sums * scale).astype(bf16)
+    else:
+        scratch[...] = sums * scale
+        rows = carried[0].shape[0]
+        for ref, part in zip(carried, (key[1], 1 - key[1])):
+            ref[...] = scratch[pl.ds(pl.multiple_of(part * rows, rows), rows), :].astype(bf16)
+
+
+def level_two(key, pre, up, picked, front, before, scale, rate, groups):
     chunk, tok = pre.shape
     cols = picked.shape[0]
     step = min(math.gcd(chunk, 256), tok)
     return kernel_call(
         functools.partial(slope_kernel, scale, rate, step, groups),
-        [((cols, tok), bf16), ((1, tok), f32)]
+        ([((cols, tok), bf16)] if groups > 1 else [((cols // 2, tok), bf16)] * 2)
+        + [((1, tok), f32)]
         + [((cols // groups, chunk), bf16 if groups > 1 else f32)] * groups,
-        [pre, up, picked, front] + before,
+        [key, pre, up, picked, front] + before,
         flops=4 * tok * cols * chunk,
+        scratch=[pltpu.VMEM((cols, tok), f32)],
         exps=tok * chunk,
     )
 
@@ -188,6 +215,24 @@
 
 def add_up(pieces):
     return kernel_call(add_kernel, [(pieces[0].shape, bf16)], pieces)[0]
+
+
+def half_kernel(key, *refs):
+    halves, (whole, out, total) = refs[:-3], refs[-3:]
+    rows = halves[0].shape[0]
+    at = pl.ds(pl.multiple_of(key[1] * rows, rows), rows)
+    total[...] = whole[...].astype(f32)
+    add = halves[0][...].astype(f32)
+    for half in halves[1:]:
+        add += half[...].astype(f32)
+    total[at, :] += add
+    out[...] = total[...].astype(bf16)
+
+
+def add_half(key, pieces):
+    shape = pieces[-1].shape
+    scratch = [pltpu.VMEM(shape, f32)]
+    return kernel_call(half_kernel, [(shape, bf16)], [key] + pieces, scratch=scratch)[0]
 
 
 def back_kernel(share, mine, theirs, stream, rate, *groups):
@@ -206,21 +251,6 @@
     )
 
 
-def outer_kernel(key, piece, moment, *refs):
-    deltas, (fresh, moment_new) = refs[:-2], refs[-2:]
-    chunk = deltas[0].shape[1]
-    for m, delta in enumerate(deltas):
-        at = pl.ds(pl.multiple_of((m ^ key[0]) * chunk, chunk), chunk)
-        fresh[:, at], moment_new[:, at] = updated(
-            piece[:, at], moment[:, at], delta[...].astype(f32)
-        )
-
-
-def outer_chunks(key, piece, moment, deltas):
-    outs = [(piece.shape, f32)] * 2
-    return kernel_call(outer_kernel, outs, [key, piece, moment] + deltas)
-
-
 def hold_kernel(*refs):
     out, start = refs[-1], 0
     for piece in refs[:-1]:
@@ -233,25 +263,73 @@
     return kernel_call(hold_kernel, [((rows, pieces[0].shape[1]), bf16)], pieces)[0]
 
 
+def part_kernel(*refs):
+    groups, (acts, out) = refs[:-2], refs[-2:]
+    group = jnp.concatenate([g[...] for g in groups], axis=1)
+    out[...] = jnp.dot(group, acts[: group.shape[1], :], preferred_element_type=f32)
+
+
+def first_part(groups, acts):
+    share, hid = groups[0].shape[0], acts.shape[1]
+    outs = [((share, hid), f32)]
+    flops = 2 * len(groups) * groups[0].size * hid
+    return kernel_call(part_kernel, outs, groups + [acts], flops=flops)[0]
+
+
+def put_out(deltas, steps, piece, moment, outs, bufs, sem):
+    copies = []
+    for i, at in enumerate(steps):
+        for buf, value in zip(bufs, updated(piece[:, at], moment[:, at], deltas(i, at))):
+            buf[:, at] = value
+        for o, (buf, out) in enumerate(zip(bufs, outs)):
+            copies.append(pltpu.make_async_copy(buf.at[:, at], out.at[:, at], sem.at[o, i]))
+            copies[-1].start()
+    for copy in copies:
+        copy.wait()
+
+
 def finish_kernel(step, *refs):
-    groups, (acts, piece, moment, fresh, moment_new) = refs[:-5], refs[-5:]
+    refs, (fresh, moment_new, *bufs, sem) = refs[:-5], refs[-5:]
+    groups, (acts, done, piece, moment) = refs[:-4], refs[-4:]
     group = jnp.concatenate([g[...] for g in groups], axis=1)
-
-    @pl.loop(0, piece.shape[1] // step)
-    def _(i):
-        at = pl.ds(pl.multiple_of(i * step, step), step)
-        delta = jnp.dot(group, acts[:, at], preferred_element_type=f32)
-        fresh[:, at], moment_new[:, at] = updated(piece[:, at], moment[:, at], delta)
-
-
-def finish(groups, acts, piece, moment):
-    share, hid = piece.shape
+    start = acts.shape[0] - group.shape[1]
+
+    def delta(i, at):
+        return done[:, at] + jnp.dot(group, acts[start:, at], preferred_element_type=f32)
+
+    steps = [pl.ds(i, step) for i in range(0, piece.shape[1], step)]
+    put_out(delta, steps, piece, moment, (fresh, moment_new), bufs, sem)
+
+
+def outer_args(shape, count):
+    scratch = [pltpu.VMEM(shape, f32)] * 2 + [pltpu.SemaphoreType.DMA((2, count))]
+    return dict(outs=[(shape, f32)] * 2, scratch=scratch, outs_in=pl.ANY)
+
+
+def finish(groups, acts, done, piece, moment):
+    _, hid = piece.shape
+    step = math.gcd(hid, 1024)
     return kernel_call(
-        functools.partial(finish_kernel, math.gcd(hid, 1024)),
-        [((share, hid), f32)] * 2,
-        groups + [acts, piece, moment],
-        flops=2 * share * hid * acts.shape[0],
+        functools.partial(finish_kernel, step),
+        args=groups + [acts, done, piece, moment],
+        flops=2 * len(groups) * groups[0].size * hid,
+        **outer_args(piece.shape, hid // step),
     )
+
+
+def outer_kernel(key, piece, moment, *refs):
+    deltas, (fresh, moment_new, *bufs, sem) = refs[:-5], refs[-5:]
+    chunk = deltas[0].shape[1]
+    steps = [
+        pl.ds(pl.multiple_of((m ^ key[0]) * chunk, chunk), chunk) for m in range(len(deltas))
+    ]
+    delta = lambda i, at: deltas[i][...].astype(f32)
+    put_out(delta, steps, piece, moment, (fresh, moment_new), bufs, sem)
+
+
+def outer_chunks(key, piece, moment, deltas):
+    args = [key, piece, moment] + deltas
+    return kernel_call(outer_kernel, args=args, **outer_args(piece.shape, len(deltas)))
 
 
 def on_device(
@@ -286,8 +364,8 @@
 
     farthest = sorted(range(1, n_c), reverse=True)
     sent = [part(second_store, c ^ m, chunk, 0) for m in farthest]
+    act_out = after(act, *sent)
     weights = {m: swap(piece, "col", m) for m, piece in zip(farthest, sent)}
-    act_out = after(act, *sent)
     mine = after(residual[0, 0], *sent)
     resid_all = [swap(mine, "tp", t) for t in range(n_t)]
     gate = resid_all[-1]
@@ -327,8 +405,9 @@
     stream_rows = jnp.concatenate(
         arrange([stream_rows[j * share : (j + 1) * share] for j in range(n_r)], r), axis=0
     )
-    piece_one = after(first_store, gate)[:, :share].T
-    piece_two = after(second_store, gate)[:, :share].T
+    first = (lambda x: lead(x, share)) if kernels else (lambda x: x[:, :share].T)
+    piece_one = first(after(first_store, gate))
+    piece_two = first(after(second_store, gate))
     ready = [weights[0], stream_rows, piece_one, piece_two] + resid + sent_ups
 
     mine = []
@@ -378,7 +457,9 @@
             pre, front = pre_second(
                 key, streams[0], streams[1], pieces, share, scale_model
             )
-            carried, *sums = level_two(
+            last = m == n_c - 1
+            found = level_two(
+                key,
                 pre,
                 ups[m],
                 picked,
@@ -386,9 +467,13 @@
                 sums,
                 scale_model,
                 inner_rate * scale_model,
-                n_c if m == n_c - 1 else 1,
+                n_c if last else 1,
             )
-            grad_two = sums[1:]
+            if last:
+                carried, grad_two = found[0], found[2:]
+            else:
+                sums = list(found[2:])
+                carried = add_up([found[0], swap(found[1], "tp", 1)])
         else:
             around = arrange([s.reshape(tok, n_r, sub) for s in streams], k)
             stream = jnp.stack(around, axis=2).reshape(tok, wide)
@@ -408,7 +493,7 @@
 
     rate = weight_row[0] * (inner_rate * scale_hidden) / total_one
     if kernels:
-        partial_value = add_up(arrived)
+        partial_value = add_half(key, arrived)
         theirs = swap(partial_value, "tp", 1)
         groups = back_groups(partial_value, theirs, stream_rows, rate, share)
     else:
@@ -426,7 +511,8 @@
         held = hold([a for j in range(n_r) for a in acts[j]])
         own_key = jnp.stack([c, k]).astype(jnp.int32)
         fresh_two = outer_chunks(own_key, piece_two, moment_two, deltas)
-        fresh_one = finish(groups, held, piece_one, moment_one)
+        done = first_part(groups[:1], held)
+        fresh_one = finish(groups[1:], held, done, piece_one, moment_one)
     else:
         delta_two = jnp.concatenate(arrange(deltas, c), axis=1).astype(f32)
         fresh_two = updated(piece_two, moment_two, delta_two)

time: 240 us -> 240 us (level)
  local copies, waits for them, and re-layouts: 37.8 us -> 17.7 us
  Pallas kernels: 26 us -> 36.6 us
  waiting for transfers between devices: 101 us -> 110 us
    unnamed x50 -> x46, local copies, waits for them, and re-layouts: 23.4 us -> 9.93 us
    pallas_call x0 -> x2, Pallas kernels: none -> 10.6 us  [lead(): pl.pallas_call(functools.partial(lead_kernel, share), grid=(hid // step,)...]
    ppermute x38 -> x41, waiting for transfers between devices: 101 us -> 110 us  [swap(): return lax.ppermute(values, axis, [(i, i ^ step) for i in range(count)])]
    transpose x2 -> x0, local copies, waits for them, and re-layouts: 3.96 us -> none  [the longest x1 2.04 us: on_device(): piece_two = after(second_store, gate)[:, :share].T]
    dynamic_slice x7 -> x6, local copies, waits for them, and re-layouts: 7.8 us -> 5.15 us  [part(): return lax.dynamic_slice_in_dim(values, index * size, size, dim)]
    ppermute x38 -> x41, starting transfers between devices: 56 us -> 56.8 us  [swap(): return lax.ppermute(values, axis, [(i, i ^ step) for i in range(count)])]
    pallas_call x15 -> x19, Pallas kernels: 26 us -> 26 us  [kernel_call(): pl.pallas_call(kernel, in_specs=[smem if x.size < 16 else vmem for x in a...]
  transfers between devices with their start and end apart: 38 -> 41, of which waited for: 14 -> 16; matrix products, arithmetic and copies ran while one was open for 18% -> 9% of each run, Pallas kernels for 9% -> 14%
where the time goes in v1:
time: 240 us; the launch traced here: 239 us
  waiting for transfers between devices  110 us (46%)
  starting transfers between devices  56.8 us (24%)
  Pallas kernels  36.6 us (15%)
  local copies, waits for them, and re-layouts  17.7 us (7%)
  matrix products  11.3 us (5%)
  between operations  3.84 us (2%)
  other arithmetic  2.98 us (1%)
    ppermute x41, waiting for transfers between devices, swap(): return lax.ppermute(values, axis, [(i, i ^ step) for i in range(count)])  110 us
    ppermute x41, starting transfers between devices, swap(): return lax.ppermute(values, axis, [(i, i ^ step) for i in range(count)])  56.8 us
    pallas_call x19, Pallas kernels, kernel_call(): pl.pallas_call(kernel, in_specs=[smem if x.size < 16 else vmem for x in a...  26 us
    dot_general x5, matrix products, on_device(): jnp.dot(after(a, *behind), first_store, preferred_element_type=f32)  11.3 us
    pallas_call x2, Pallas kernels, lead(): pl.pallas_call(functools.partial(lead_kernel, share), grid=(hid // step,)...  10.6 us
    unnamed x46, local copies, waits for them, and re-layouts  9.93 us
    dynamic_slice x6, local copies, waits for them, and re-layouts, part(): return lax.dynamic_slice_in_dim(values, index * size, size, dim)  5.15 us
  transfers between devices with their start and end apart: 41, of which 16 were waited for; matrix products, arithmetic and copies ran while one was open for 9% of the time, Pallas kernels for 14%

profile of v1, /device:TPU:0, one launch (start us, length us, event | category | flops | bytes accessed | tf_op | source)
XLA Modules:
  0.0 239.1 jit_solution(15409536578216144332)
XLA Ops:
  0.7 3.7 %dynamic-slice_bitcast_fusion = (bf16[1024,512]{1,0:T(8,128)(2,1)}, bf16[1024,512]{1,0:T(8,128)(2,1)}, bf16[1024,512]{1,0:T(8,128)(2,1)}) fusion(bf16[1,4096,512]{2,1,0:T(8,128)(2,1)} %param.17, s32[]{:T(128)S(6)} %select_n.132, s32[]{:T(128)S(6)} %select_n.131, s32[]{:T(128)S(6)} %select_n.130), kind=kLoop, calls=%fused_computation.19 | loop fusion | bytes 6291468 | tf_op jit(solution)/shard_map/dynamic_slice | solution.py:42
  4.8 2.5 %collective-permute-start.2 = (bf16[256,4096]{1,0:T(8,128)(2,1)}, bf16[256,4096]{1,0:T(8,128)(2,1)}, u32[]{:S(2)}, u32[]{:S(2)}) collective-permute-start(bf16[256,4096]{1,0:T(8,128)(2,1)} %bitcast.12.refs_0_), channel_id=1, source_target_pairs={{0,8},{8,0},{16,24},{24,16},{1,9},{9,1},{17,25},{25,17},{2,10},{10... | collective-permute-start | bytes 6291464 | tf_op jit(solution)/shard_map/ppermute | solution.py:25
  10.4 2.6 %collective-permute-start.14 = (bf16[1024,512]{1,0:T(8,128)(2,1)}, bf16[1024,512]{1,0:T(8,128)(2,1)S(1)}, u32[]{:S(2)}, u32[]{:S(2)}) collective-permute-start(bf16[1024,512]{1,0:T(8,128)(2,1)} %get-tuple-element.97), channel_id=1, source_target_pairs={{0,4},{2,6},{4,0},{6,2},{1,5},{3,7},{5,1},{7,3},{8,12},{10,14},{12... | collective-permute-start | bytes 3145736 | tf_op jit(solution)/shard_map/ppermute | solution.py:25
  13.1 4.1 %copy.15 = bf16[1,1,256,4096]{2,3,1,0:T(8,128)(2,1)} copy(bf16[1,1,256,4096]{3,2,1,0:T(8,128)(2,1)} %param.12) | data formatting | bytes 4194304 | tf_op args[2]
  18.0 4.1 %fusion = bf16[256,512]{1,0:T(8,128)(2,1)S(1)} fusion(bf16[256,4096]{1,0:T(8,128)(2,1)} %bitcast.12.refs_0_, bf16[1,4096,512]{2,1,0:T(8,128)(2,1)} %param.16), kind=kOutput, calls=%fused_computation.12 | convolution fusion | flops 1074003968 | bytes 6553600 | tf_op jit(solution)/shard_map/dot_general | solution.py:417
  22.1 5.3 %lead.2.refs_5_ = bf16[64,4096]{1,0:T(8,128)(2,1)} custom-call(bf16[4096,512]{1,0:T(8,128)(2,1)} %bitcast.76), custom_call_target="tpu_custom_call" | custom-call | tf_op jit(solution)/shard_map/lead/pallas_call | solution.py:116
  27.4 5.3 %lead.3.piece = bf16[64,4096]{1,0:T(8,128)(2,1)} custom-call(bf16[4096,512]{1,0:T(8,128)(2,1)} %bitcast.77), custom_call_target="tpu_custom_call" | custom-call | tf_op jit(solution)/shard_map/lead/pallas_call | solution.py:116
  36.8 17.1 %collective-permute-done.2.refs_1_ = bf16[256,4096]{1,0:T(8,128)(2,1)} collective-permute-done((bf16[256,4096]{1,0:T(8,128)(2,1)}, bf16[256,4096]{1,0:T(8,128)(2,1)}, u32[]{:S(2)}, u32[]{:S(2)}) %collective-permute-start.2) | collective-permute-done | bytes 2097184 | tf_op jit(solution)/shard_map/ppermute | solution.py:25
  57.1 2.8 %fusion.1 = bf16[256,512]{1,0:T(8,128)(2,1)S(1)} fusion(bf16[256,4096]{1,0:T(8,128)(2,1)} %collective-permute-done.2.refs_1_, bf16[1,4096,512]{2,1,0:T(8,128)(2,1)S(1)} %copy-done.16), kind=kOutput, calls=%fused_computation.13 | convolution fusion | flops 1074003968 | bytes 6553600 | tf_op jit(solution)/shard_map/dot_general | solution.py:417
  63.1 2.8 %fusion.2 = bf16[256,512]{1,0:T(8,128)(2,1)S(1)} fusion(bf16[256,4096]{1,0:T(8,128)(2,1)} %collective-permute-done.5.refs_2_, bf16[1,4096,512]{2,1,0:T(8,128)(2,1)S(1)} %copy-done.16), kind=kOutput, calls=%fused_computation.14 | convolution fusion | flops 1074003968 | bytes 6553600 | tf_op jit(solution)/shard_map/dot_general | solution.py:417
  66.0 3.7 %collective-permute-start.15 = (bf16[1024,512]{1,0:T(8,128)(2,1)S(1)}, bf16[1024,512]{1,0:T(8,128)(2,1)S(1)}, u32[]{:S(2)}, u32[]{:S(2)}) collective-permute-start(bf16[1024,512]{1,0:T(8,128)(2,1)S(1)} %copy-done.18), channel_id=1, source_target_pairs={{0,6},{2,4},{4,2},{6,0},{1,7},{3,5},{5,3},{7,1},{8,14},{10,12},{12... | collective-permute-start | bytes 3145736 | tf_op jit(solution)/shard_map/ppermute | solution.py:25
  69.7 11.5 %collective-permute-done.8.refs_3_ = bf16[128,4096]{1,0:T(8,128)(2,1)S(1)} collective-permute-done((bf16[128,4096]{1,0:T(8,128)(2,1)S(1)}, bf16[128,4096]{1,0:T(8,128)(2,1)S(1)}, u32[]{:S(2)}, u32[]{:S(2)}) %collective-permute-start.8) | collective-permute-done | bytes 1048608 | tf_op jit(solution)/shard_map/ppermute | solution.py:25
  82.1 4.8 %collective-permute-done.9.refs_4_ = bf16[128,4096]{1,0:T(8,128)(2,1)S(1)} collective-permute-done((bf16[128,4096]{1,0:T(8,128)(2,1)S(1)}, bf16[128,4096]{1,0:T(8,128)(2,1)S(1)}, u32[]{:S(2)}, u32[]{:S(2)}) %collective-permute-start.9) | collective-permute-done | bytes 1048608 | tf_op jit(solution)/shard_map/ppermute | solution.py:25
  93.0 2.2 collective-permute-done.4.refs_5_
  95.2 2.6 %collective-permute-start.11 = (bf16[256,256]{1,0:T(8,128)(2,1)S(1)}, bf16[256,256]{1,0:T(8,128)(2,1)S(1)}, u32[]{:S(2)}, u32[]{:S(2)}) collective-permute-start(bf16[256,256]{1,0:T(8,128)(2,1)S(1)} %add_convert_fusion), channel_id=1, source_target_pairs={{0,24},{8,16},{16,8},{24,0},{1,25},{9,17},{17,9},{25,1},{2,26},{10... | collective-permute-start | bytes 393224 | tf_op jit(solution)/shard_map/ppermute | solution.py:25
  97.9 3.2 %collective-permute-done.11.refs_7_ = bf16[256,256]{1,0:T(8,128)(2,1)S(1)} collective-permute-done((bf16[256,256]{1,0:T(8,128)(2,1)S(1)}, bf16[256,256]{1,0:T(8,128)(2,1)S(1)}, u32[]{:S(2)}, u32[]{:S(2)}) %collective-permute-start.11) | collective-permute-done | bytes 131104 | tf_op jit(solution)/shard_map/ppermute | solution.py:25
  101.2 2.8 %collective-permute-start.22 = (bf16[256,1024]{1,0:T(8,128)(2,1)S(1)}, bf16[256,1024]{1,0:T(8,128)(2,1)}, u32[]{:S(2)}, u32[]{:S(2)}) collective-permute-start(bf16[256,1024]{1,0:T(8,128)(2,1)S(1)} %shard_map.129.same), channel_id=1, source_target_pairs={{0,4},{2,6},{4,0},{6,2},{1,5},{3,7},{5,1},{7,3},{8,12},{10,14},{12... | collective-permute-start | bytes 1572872 | tf_op jit(solution)/shard_map/ppermute | solution.py:25
  106.5 30.9 %collective-permute-done.22.same = bf16[256,1024]{1,0:T(8,128)(2,1)} collective-permute-done((bf16[256,1024]{1,0:T(8,128)(2,1)S(1)}, bf16[256,1024]{1,0:T(8,128)(2,1)}, u32[]{:S(2)}, u32[]{:S(2)}) %collective-permute-start.22) | collective-permute-done | bytes 524320 | tf_op jit(solution)/shard_map/ppermute | solution.py:25
  142.8 21.2 %collective-permute-done.27.same = bf16[256,1024]{1,0:T(8,128)(2,1)} collective-permute-done((bf16[256,1024]{1,0:T(8,128)(2,1)}, bf16[256,1024]{1,0:T(8,128)(2,1)}, u32[]{:S(2)}, u32[]{:S(2)}) %collective-permute-start.27) | collective-permute-done | bytes 524320 | tf_op jit(solution)/shard_map/ppermute | solution.py:25
  163.9 2.5 %collective-permute-start.29 = (bf16[1040,256]{1,0:T(8,128)(2,1)}, bf16[1040,256]{1,0:T(8,128)(2,1)S(1)}, u32[]{:S(2)}, u32[]{:S(2)}) collective-permute-start(bf16[1040,256]{1,0:T(8,128)(2,1)} %get-tuple-element.111), channel_id=1, source_target_pairs={{0,6},{2,4},{4,2},{6,0},{1,7},{3,5},{5,3},{7,1},{8,14},{10,12},{12... | collective-permute-start | bytes 1597448 | tf_op jit(solution)/shard_map/ppermute | solution.py:25
  172.4 2.7 %shard_map.134 = (f32[1024,256]{1,0:T(8,128)S(1)}, bf16[256,256]{1,0:T(8,128)(2,1)S(1)}) custom-call(s32[2]{0:T(128)S(1)} %pad_add_fusion.key, bf16[256,1024]{1,0:T(8,128)(2,1)} %collective-permute-done.17.same, bf16[256,1024]{1,0:T(8,128)(2,1)} %collective-permute-done.18.other, bf16[1024,512]{1,0:T(8,128)(2,1)S(1)} %constant_dynamic-slice_fusion.2.refs_0_, ...), custom_call_target="tpu_custom_call" | custom-call | flops 1073741824 | bytes 6422536 | tf_op jit(solution)/shard_map/pallas_call | solution.py:67
  177.0 2.7 %shard_map.137 = (f32[1024,256]{1,0:T(8,128)S(1)}, bf16[256,256]{1,0:T(8,128)(2,1)S(1)}) custom-call(s32[2]{0:T(128)S(1)} %pad_add_fusion.key, bf16[256,1024]{1,0:T(8,128)(2,1)} %collective-permute-done.22.same, bf16[256,1024]{1,0:T(8,128)(2,1)} %collective-permute-done.23.other, bf16[1024,512]{1,0:T(8,128)(2,1)S(1)} %constant_dynamic-slice_fusion.2.refs_0_, ...), custom_call_target="tpu_custom_call" | custom-call | flops 1073741824 | bytes 6422536 | tf_op jit(solution)/shard_map/pallas_call | solution.py:67
  181.7 2.8 %shard_map.140 = (f32[1024,256]{1,0:T(8,128)S(1)}, bf16[256,256]{1,0:T(8,128)(2,1)S(1)}) custom-call(s32[2]{0:T(128)S(1)} %pad_add_fusion.key, bf16[256,1024]{1,0:T(8,128)(2,1)} %collective-permute-done.27.same, bf16[256,1024]{1,0:T(8,128)(2,1)} %collective-permute-done.28.other, bf16[1024,512]{1,0:T(8,128)(2,1)S(1)} %constant_dynamic-slice_fusion.2.refs_0_, ...), custom_call_target="tpu_custom_call" | custom-call | flops 1073741824 | bytes 6422536 | tf_op jit(solution)/shard_map/pallas_call | solution.py:67
  187.5 11.2 %collective-permute-start.30 = (bf16[256,256]{1,0:T(8,128)(2,1)S(1)}, bf16[256,256]{1,0:T(8,128)(2,1)S(1)}, u32[]{:S(2)}, u32[]{:S(2)}) collective-permute-start(bf16[256,256]{1,0:T(8,128)(2,1)S(1)} %get-tuple-element.82), channel_id=1, source_target_pairs={{0,6},{2,4},{4,2},{6,0},{1,7},{3,5},{5,3},{7,1},{8,14},{10,12},{12... | collective-permute-start | bytes 393224 | tf_op jit(solution)/shard_map/ppermute | solution.py:25
  201.0 2.8 %collective-permute-done.21.refs_1_ = bf16[128,256]{1,0:T(8,128)(2,1)S(1)} collective-permute-done((bf16[128,256]{1,0:T(8,128)(2,1)S(1)}, bf16[128,256]{1,0:T(8,128)(2,1)S(1)}, u32[]{:S(2)}, u32[]{:S(2)}) %collective-permute-start.21) | collective-permute-done | bytes 65568 | tf_op jit(solution)/shard_map/ppermute | solution.py:25
  203.8 4.2 %collective-permute-done.26.refs_2_ = bf16[128,256]{1,0:T(8,128)(2,1)S(1)} collective-permute-done((bf16[128,256]{1,0:T(8,128)(2,1)S(1)}, bf16[128,256]{1,0:T(8,128)(2,1)S(1)}, u32[]{:S(2)}, u32[]{:S(2)}) %collective-permute-start.26) | collective-permute-done | bytes 65568 | tf_op jit(solution)/shard_map/ppermute | solution.py:25
  209.2 3.4 %collective-permute-start.39 = (bf16[64,1024]{1,0:T(8,128)(2,1)S(1)}, bf16[64,1024]{1,0:T(8,128)(2,1)S(1)}, u32[]{:S(2)}, u32[]{:S(2)}) collective-permute-start(bf16[64,1024]{1,0:T(8,128)(2,1)S(1)} %get-tuple-element.92), channel_id=1, source_target_pairs={{0,4},{2,6},{4,0},{6,2},{1,5},{3,7},{5,1},{7,3},{8,12},{10,14},{12... | collective-permute-start | bytes 393224 | tf_op jit(solution)/shard_map/ppermute | solution.py:25
  214.7 2.3 collective-permute-done.32
  218.1 2.7 %collective-permute-done.33 = s32[1]{0:T(128)} collective-permute-done((s32[1]{0:T(128)}, s32[1]{0:T(128)}, u32[]{:S(2)}, u32[]{:S(2)}) %collective-permute-start.33) | collective-permute-done | bytes 36 | tf_op jit(solution)/shard_map/ppermute | solution.py:25
  222.9 2.6 %collective-permute-done.34 = s32[1]{0:T(128)} collective-permute-done((s32[1]{0:T(128)}, s32[1]{0:T(128)}, u32[]{:S(2)}, u32[]{:S(2)}) %collective-permute-start.34) | collective-permute-done | bytes 36 | tf_op jit(solution)/shard_map/ppermute | solution.py:25
  229.8 3.5 %shard_map.144.refs_1_.refs_3_ = bf16[1024,4096]{1,0:T(8,128)(2,1)S(1)} custom-call(bf16[256,4096]{1,0:T(8,128)(2,1)} %bitcast.12.refs_0_, bf16[256,4096]{1,0:T(8,128)(2,1)} %collective-permute-done.2.refs_1_, bf16[256,4096]{1,0:T(8,128)(2,1)} %collective-permute-done.5.refs_2_, bf16[128,4096]{1,0:T(8,128)(2,1)S(1)} %copy-done.4, bf16[128,4096]{1,0:T(8,128)(2,1)S(1)} %copy-done.6), custom_call_target="tpu_custom_call" | custom-call | bytes 16777216 | tf_op jit(solution)/shard_map/pallas_call | solution.py:67
  236.8 2.2 shard_map.146
  (146 shorter events, 56.6 us)
Async XLA Ops:
  4.3 13.7 %collective-permute-start = (bf16[256,1024]{1,0:T(8,128)(2,1)S(1)}, bf16[256,1024]{1,0:T(8,128)(2,1)S(1)}, u32[]{:S(2)}, u32[]{:S(2)}) collective-permute-start(bf16[256,1024]{1,0:T(8,128)(2,1)S(1)} %bitcast.80), channel_id=1, source_target_pairs={{0,1},{1,0},{2,3},{3,2},{4,5},{5,4},{6,7},{7,6},{8,9},{9,8},{10,11... | collective-permute-start | bytes 1572872 | tf_op jit(solution)/shard_map/ppermute | solution.py:25
  4.8 49.1 %collective-permute-start.2 = (bf16[256,4096]{1,0:T(8,128)(2,1)}, bf16[256,4096]{1,0:T(8,128)(2,1)}, u32[]{:S(2)}, u32[]{:S(2)}) collective-permute-start(bf16[256,4096]{1,0:T(8,128)(2,1)} %bitcast.12.refs_0_), channel_id=1, source_target_pairs={{0,8},{8,0},{16,24},{24,16},{1,9},{9,1},{17,25},{25,17},{2,10},{10... | collective-permute-start | bytes 6291464 | tf_op jit(solution)/shard_map/ppermute | solution.py:25
  7.3 48.1 %collective-permute-start.5 = (bf16[256,4096]{1,0:T(8,128)(2,1)}, bf16[256,4096]{1,0:T(8,128)(2,1)}, u32[]{:S(2)}, u32[]{:S(2)}) collective-permute-start(bf16[256,4096]{1,0:T(8,128)(2,1)} %bitcast.12.refs_0_), channel_id=1, source_target_pairs={{0,16},{8,24},{16,0},{24,8},{1,17},{9,25},{17,1},{25,9},{2,18},{10... | collective-permute-start | bytes 6291464 | tf_op jit(solution)/shard_map/ppermute | solution.py:25
  8.8 96.8 %collective-permute-start.13 = (bf16[1024,512]{1,0:T(8,128)(2,1)}, bf16[1024,512]{1,0:T(8,128)(2,1)S(1)}, u32[]{:S(2)}, u32[]{:S(2)}) collective-permute-start(bf16[1024,512]{1,0:T(8,128)(2,1)} %get-tuple-element.96), channel_id=1, source_target_pairs={{0,2},{2,0},{4,6},{6,4},{1,3},{3,1},{5,7},{7,5},{8,10},{10,8},{12,... | collective-permute-start | bytes 3145736 | tf_op jit(solution)/shard_map/ppermute | solution.py:25
  10.4 127.0 %collective-permute-start.14 = (bf16[1024,512]{1,0:T(8,128)(2,1)}, bf16[1024,512]{1,0:T(8,128)(2,1)S(1)}, u32[]{:S(2)}, u32[]{:S(2)}) collective-permute-start(bf16[1024,512]{1,0:T(8,128)(2,1)} %get-tuple-element.97), channel_id=1, source_target_pairs={{0,4},{2,6},{4,0},{6,2},{1,5},{3,7},{5,1},{7,3},{8,12},{10,14},{12... | collective-permute-start | bytes 3145736 | tf_op jit(solution)/shard_map/ppermute | solution.py:25
  56.7 24.5 %collective-permute-start.8 = (bf16[128,4096]{1,0:T(8,128)(2,1)S(1)}, bf16[128,4096]{1,0:T(8,128)(2,1)S(1)}, u32[]{:S(2)}, u32[]{:S(2)}) collective-permute-start(bf16[128,4096]{1,0:T(8,128)(2,1)S(1)} %slice.28), channel_id=1, source_target_pairs={{0,8},{8,0},{16,24},{24,16},{1,9},{9,1},{17,25},{25,17},{2,10},{10... | collective-permute-start | bytes 3145736 | tf_op jit(solution)/shard_map/ppermute | solution.py:25
  60.0 6.0 %collective-permute-start.3 = (bf16[256,256]{1,0:T(8,128)(2,1)S(1)}, bf16[256,256]{1,0:T(8,128)(2,1)S(1)}, u32[]{:S(2)}, u32[]{:S(2)}) collective-permute-start(bf16[256,256]{1,0:T(8,128)(2,1)S(1)} %constant_dynamic-slice_fusion.1), channel_id=1, source_target_pairs={{0,1},{1,0},{2,3},{3,2},{4,5},{5,4},{6,7},{7,6},{8,9},{9,8},{10,11... | collective-permute-start | bytes 393224 | tf_op jit(solution)/shard_map/ppermute | solution.py:25
  61.3 25.6 %collective-permute-start.9 = (bf16[128,4096]{1,0:T(8,128)(2,1)S(1)}, bf16[128,4096]{1,0:T(8,128)(2,1)S(1)}, u32[]{:S(2)}, u32[]{:S(2)}) collective-permute-start(bf16[128,4096]{1,0:T(8,128)(2,1)S(1)} %slice.29), channel_id=1, source_target_pairs={{0,16},{8,24},{16,0},{24,8},{1,17},{9,25},{17,1},{25,9},{2,18},{10... | collective-permute-start | bytes 3145736 | tf_op jit(solution)/shard_map/ppermute | solution.py:25
  66.0 73.5 %collective-permute-start.15 = (bf16[1024,512]{1,0:T(8,128)(2,1)S(1)}, bf16[1024,512]{1,0:T(8,128)(2,1)S(1)}, u32[]{:S(2)}, u32[]{:S(2)}) collective-permute-start(bf16[1024,512]{1,0:T(8,128)(2,1)S(1)} %copy-done.18), channel_id=1, source_target_pairs={{0,6},{2,4},{4,2},{6,0},{1,7},{3,5},{5,3},{7,1},{8,14},{10,12},{12... | collective-permute-start | bytes 3145736 | tf_op jit(solution)/shard_map/ppermute | solution.py:25
  81.2 10.2 %collective-permute-start.1 = (bf16[256,256]{1,0:T(8,128)(2,1)S(1)}, bf16[256,256]{1,0:T(8,128)(2,1)S(1)}, u32[]{:S(2)}, u32[]{:S(2)}) collective-permute-start(bf16[256,256]{1,0:T(8,128)(2,1)S(1)} %constant_dynamic-slice_fusion.3), channel_id=1, source_target_pairs={{0,1},{1,0},{2,3},{3,2},{4,5},{5,4},{6,7},{7,6},{8,9},{9,8},{10,11... | collective-permute-start | bytes 393224 | tf_op jit(solution)/shard_map/ppermute | solution.py:25
  91.4 6.5 %collective-permute-start.7 = (bf16[256,256]{1,0:T(8,128)(2,1)S(1)}, bf16[256,256]{1,0:T(8,128)(2,1)S(1)}, u32[]{:S(2)}, u32[]{:S(2)}) collective-permute-start(bf16[256,256]{1,0:T(8,128)(2,1)S(1)} %add_convert_fusion.1), channel_id=1, source_target_pairs={{0,16},{8,24},{16,0},{24,8},{1,17},{9,25},{17,1},{25,9},{2,18},{10... | collective-permute-start | bytes 393224 | tf_op jit(solution)/shard_map/ppermute | solution.py:25
  101.2 36.2 %collective-permute-start.22 = (bf16[256,1024]{1,0:T(8,128)(2,1)S(1)}, bf16[256,1024]{1,0:T(8,128)(2,1)}, u32[]{:S(2)}, u32[]{:S(2)}) collective-permute-start(bf16[256,1024]{1,0:T(8,128)(2,1)S(1)} %shard_map.129.same), channel_id=1, source_target_pairs={{0,4},{2,6},{4,0},{6,2},{1,5},{3,7},{5,1},{7,3},{8,12},{10,14},{12... | collective-permute-start | bytes 1572872 | tf_op jit(solution)/shard_map/ppermute | solution.py:25
  104.1 33.4 %collective-permute-start.17 = (bf16[256,1024]{1,0:T(8,128)(2,1)S(1)}, bf16[256,1024]{1,0:T(8,128)(2,1)}, u32[]{:S(2)}, u32[]{:S(2)}) collective-permute-start(bf16[256,1024]{1,0:T(8,128)(2,1)S(1)} %shard_map.129.same), channel_id=1, source_target_pairs={{0,2},{2,0},{4,6},{6,4},{1,3},{3,1},{5,7},{7,5},{8,10},{10,8},{12,... | collective-permute-start | bytes 1572872 | tf_op jit(solution)/shard_map/ppermute | solution.py:25
  105.6 35.0 %collective-permute-start.12 = (bf16[256,1024]{1,0:T(8,128)(2,1)S(1)}, bf16[256,1024]{1,0:T(8,128)(2,1)S(1)}, u32[]{:S(2)}, u32[]{:S(2)}) collective-permute-start(bf16[256,1024]{1,0:T(8,128)(2,1)S(1)} %shard_map.129.same), channel_id=1, source_target_pairs={{0,1},{1,0},{2,3},{3,2},{4,5},{5,4},{6,7},{7,6},{8,9},{9,8},{10,11... | collective-permute-start | bytes 1572872 | tf_op jit(solution)/shard_map/ppermute | solution.py:25
  137.4 26.5 %collective-permute-start.27 = (bf16[256,1024]{1,0:T(8,128)(2,1)}, bf16[256,1024]{1,0:T(8,128)(2,1)}, u32[]{:S(2)}, u32[]{:S(2)}) collective-permute-start(bf16[256,1024]{1,0:T(8,128)(2,1)} %collective-permute-done.22.same), channel_id=1, source_target_pairs={{0,2},{2,0},{4,6},{6,4},{1,3},{3,1},{5,7},{7,5},{8,10},{10,8},{12,... | collective-permute-start | bytes 1572872 | tf_op jit(solution)/shard_map/ppermute | solution.py:25
  137.4 26.5 %collective-permute-start.18 = (bf16[256,1024]{1,0:T(8,128)(2,1)}, bf16[256,1024]{1,0:T(8,128)(2,1)}, u32[]{:S(2)}, u32[]{:S(2)}) collective-permute-start(bf16[256,1024]{1,0:T(8,128)(2,1)} %collective-permute-done.17.same), channel_id=1, source_target_pairs={{0,1},{1,0},{2,3},{3,2},{4,5},{5,4},{6,7},{7,6},{8,9},{9,8},{10,11... | collective-permute-start | bytes 1572872 | tf_op jit(solution)/shard_map/ppermute | solution.py:25
  137.4 37.6 %collective-permute-start.19 = (bf16[1040,256]{1,0:T(8,128)(2,1)}, bf16[1040,256]{1,0:T(8,128)(2,1)}, u32[]{:S(2)}, u32[]{:S(2)}) collective-permute-start(bf16[1040,256]{1,0:T(8,128)(2,1)} %get-tuple-element.112), channel_id=1, source_target_pairs={{0,2},{2,0},{4,6},{6,4},{1,3},{3,1},{5,7},{7,5},{8,10},{10,8},{12,... | collective-permute-start | bytes 1597448 | tf_op jit(solution)/shard_map/ppermute | solution.py:25
  140.5 36.5 %collective-permute-start.23 = (bf16[256,1024]{1,0:T(8,128)(2,1)}, bf16[256,1024]{1,0:T(8,128)(2,1)}, u32[]{:S(2)}, u32[]{:S(2)}) collective-permute-start(bf16[256,1024]{1,0:T(8,128)(2,1)} %collective-permute-done.22.same), channel_id=1, source_target_pairs={{0,1},{1,0},{2,3},{3,2},{4,5},{5,4},{6,7},{7,6},{8,9},{9,8},{10,11... | collective-permute-start | bytes 1572872 | tf_op jit(solution)/shard_map/ppermute | solution.py:25
  141.4 38.2 %collective-permute-start.24 = (bf16[1040,256]{1,0:T(8,128)(2,1)}, bf16[1040,256]{1,0:T(8,128)(2,1)}, u32[]{:S(2)}, u32[]{:S(2)}) collective-permute-start(bf16[1040,256]{1,0:T(8,128)(2,1)} %get-tuple-element.113), channel_id=1, source_target_pairs={{0,4},{2,6},{4,0},{6,2},{1,5},{3,7},{5,1},{7,3},{8,12},{10,14},{12... | collective-permute-start | bytes 1597448 | tf_op jit(solution)/shard_map/ppermute | solution.py:25
  163.9 17.7 %collective-permute-start.28 = (bf16[256,1024]{1,0:T(8,128)(2,1)}, bf16[256,1024]{1,0:T(8,128)(2,1)}, u32[]{:S(2)}, u32[]{:S(2)}) collective-permute-start(bf16[256,1024]{1,0:T(8,128)(2,1)} %collective-permute-done.27.same), channel_id=1, source_target_pairs={{0,1},{1,0},{2,3},{3,2},{4,5},{5,4},{6,7},{7,6},{8,9},{9,8},{10,11... | collective-permute-start | bytes 1572872 | tf_op jit(solution)/shard_map/ppermute | solution.py:25
  163.9 21.9 %collective-permute-start.29 = (bf16[1040,256]{1,0:T(8,128)(2,1)}, bf16[1040,256]{1,0:T(8,128)(2,1)S(1)}, u32[]{:S(2)}, u32[]{:S(2)}) collective-permute-start(bf16[1040,256]{1,0:T(8,128)(2,1)} %get-tuple-element.111), channel_id=1, source_target_pairs={{0,6},{2,4},{4,2},{6,0},{1,7},{3,5},{5,3},{7,1},{8,14},{10,12},{12... | collective-permute-start | bytes 1597448 | tf_op jit(solution)/shard_map/ppermute | solution.py:25
  176.7 22.0 %collective-permute-start.20 = (bf16[128,256]{1,0:T(8,128)(2,1)S(1)}, bf16[128,256]{1,0:T(8,128)(2,1)S(1)}, u32[]{:S(2)}, u32[]{:S(2)}) collective-permute-start(bf16[128,256]{1,0:T(8,128)(2,1)S(1)} %get-tuple-element.71), channel_id=1, source_target_pairs={{0,1},{1,0},{2,3},{3,2},{4,5},{5,4},{6,7},{7,6},{8,9},{9,8},{10,11... | collective-permute-start | bytes 196616 | tf_op jit(solution)/shard_map/ppermute | solution.py:25
  181.3 18.6 %collective-permute-start.25 = (bf16[128,256]{1,0:T(8,128)(2,1)S(1)}, bf16[128,256]{1,0:T(8,128)(2,1)S(1)}, u32[]{:S(2)}, u32[]{:S(2)}) collective-permute-start(bf16[128,256]{1,0:T(8,128)(2,1)S(1)} %get-tuple-element.77), channel_id=1, source_target_pairs={{0,1},{1,0},{2,3},{3,2},{4,5},{5,4},{6,7},{7,6},{8,9},{9,8},{10,11... | collective-permute-start | bytes 196616 | tf_op jit(solution)/shard_map/ppermute | solution.py:25
  187.5 20.5 %collective-permute-start.30 = (bf16[256,256]{1,0:T(8,128)(2,1)S(1)}, bf16[256,256]{1,0:T(8,128)(2,1)S(1)}, u32[]{:S(2)}, u32[]{:S(2)}) collective-permute-start(bf16[256,256]{1,0:T(8,128)(2,1)S(1)} %get-tuple-element.82), channel_id=1, source_target_pairs={{0,6},{2,4},{4,2},{6,0},{1,7},{3,5},{5,3},{7,1},{8,14},{10,12},{12... | collective-permute-start | bytes 393224 | tf_op jit(solution)/shard_map/ppermute | solution.py:25
  199.9 8.1 %collective-permute-start.26 = (bf16[128,256]{1,0:T(8,128)(2,1)S(1)}, bf16[128,256]{1,0:T(8,128)(2,1)S(1)}, u32[]{:S(2)}, u32[]{:S(2)}) collective-permute-start(bf16[128,256]{1,0:T(8,128)(2,1)S(1)} %shard_map.139), channel_id=1, source_target_pairs={{0,4},{2,6},{4,0},{6,2},{1,5},{3,7},{5,1},{7,3},{8,12},{10,14},{12... | collective-permute-start | bytes 196616 | tf_op jit(solution)/shard_map/ppermute | solution.py:25
  208.6 17.5 %collective-permute-start.31 = (bf16[256,256]{1,0:T(8,128)(2,1)S(1)}, bf16[256,256]{1,0:T(8,128)(2,1)S(1)}, u32[]{:S(2)}, u32[]{:S(2)}) collective-permute-start(bf16[256,256]{1,0:T(8,128)(2,1)S(1)} %shard_map.142.mine), channel_id=1, source_target_pairs={{0,1},{1,0},{2,3},{3,2},{4,5},{5,4},{6,7},{7,6},{8,9},{9,8},{10,11... | collective-permute-start | bytes 393224 | tf_op jit(solution)/shard_map/ppermute | solution.py:25
  208.7 19.6 %collective-permute-start.38 = (bf16[64,1024]{1,0:T(8,128)(2,1)S(1)}, bf16[64,1024]{1,0:T(8,128)(2,1)S(1)}, u32[]{:S(2)}, u32[]{:S(2)}) collective-permute-start(bf16[64,1024]{1,0:T(8,128)(2,1)S(1)} %get-tuple-element.91), channel_id=1, source_target_pairs={{0,2},{2,0},{4,6},{6,4},{1,3},{3,1},{5,7},{7,5},{8,10},{10,8},{12,... | collective-permute-start | bytes 393224 | tf_op jit(solution)/shard_map/ppermute | solution.py:25
  209.2 24.2 %collective-permute-start.39 = (bf16[64,1024]{1,0:T(8,128)(2,1)S(1)}, bf16[64,1024]{1,0:T(8,128)(2,1)S(1)}, u32[]{:S(2)}, u32[]{:S(2)}) collective-permute-start(bf16[64,1024]{1,0:T(8,128)(2,1)S(1)} %get-tuple-element.92), channel_id=1, source_target_pairs={{0,4},{2,6},{4,0},{6,2},{1,5},{3,7},{5,1},{7,3},{8,12},{10,14},{12... | collective-permute-start | bytes 393224 | tf_op jit(solution)/shard_map/ppermute | solution.py:25
  212.5 20.8 %collective-permute-start.40 = (bf16[64,1024]{1,0:T(8,128)(2,1)S(1)}, bf16[64,1024]{1,0:T(8,128)(2,1)S(1)}, u32[]{:S(2)}, u32[]{:S(2)}) collective-permute-start(bf16[64,1024]{1,0:T(8,128)(2,1)S(1)} %get-tuple-element.93), channel_id=1, source_target_pairs={{0,6},{2,4},{4,2},{6,0},{1,7},{3,5},{5,3},{7,1},{8,14},{10,12},{12... | collective-permute-start | bytes 393224 | tf_op jit(solution)/shard_map/ppermute | solution.py:25
  226.2 9.7 %collective-permute-start.35 = (bf16[64,256]{1,0:T(8,128)(2,1)S(1)}, bf16[64,256]{1,0:T(8,128)(2,1)S(1)}, u32[]{:S(2)}, u32[]{:S(2)}) collective-permute-start(bf16[64,256]{1,0:T(8,128)(2,1)S(1)} %get-tuple-element.84), channel_id=1, source_target_pairs={{0,8},{8,0},{16,24},{24,16},{1,9},{9,1},{17,25},{25,17},{2,10},{10... | collective-permute-start | bytes 98312 | tf_op jit(solution)/shard_map/ppermute | solution.py:25
  227.7 8.2 %collective-permute-start.36 = (bf16[64,256]{1,0:T(8,128)(2,1)S(1)}, bf16[64,256]{1,0:T(8,128)(2,1)S(1)}, u32[]{:S(2)}, u32[]{:S(2)}) collective-permute-start(bf16[64,256]{1,0:T(8,128)(2,1)S(1)} %get-tuple-element.85), channel_id=1, source_target_pairs={{0,16},{8,24},{16,0},{24,8},{1,17},{9,25},{17,1},{25,9},{2,18},{10... | collective-permute-start | bytes 98312 | tf_op jit(solution)/shard_map/ppermute | solution.py:25
  228.3 7.6 %collective-permute-start.37 = (bf16[64,256]{1,0:T(8,128)(2,1)S(1)}, bf16[64,256]{1,0:T(8,128)(2,1)S(1)}, u32[]{:S(2)}, u32[]{:S(2)}) collective-permute-start(bf16[64,256]{1,0:T(8,128)(2,1)S(1)} %get-tuple-element.86), channel_id=1, source_target_pairs={{0,24},{8,16},{16,8},{24,0},{1,25},{9,17},{17,9},{25,1},{2,26},{10... | collective-permute-start | bytes 98312 | tf_op jit(solution)/shard_map/ppermute | solution.py:25
  (31 other events, 192.7 us)

commit v2 on v1

--- a/solution.py
+++ b/solution.py
@@ -164,10 +164,11 @@
     chunk = pre.shape[0]
     digits = up[chunk : chunk + 16, :].astype(f32)
     number = digits[0:1] + 256.0 * digits[1:2] + 65536.0 * digits[2:3]
-    seen[...] = number + before[0][...] if before else number
+    known = number + before[0][0:1] if before else number
+    seen[...] = jnp.broadcast_to(known, seen.shape)
     weight = number * rate
     if last:
-        norm = 1.0 / seen[...]
+        norm = 1.0 / known
     sums = None
     for start in range(0, chunk, step):
         rows = slice(start, start + step)
@@ -197,7 +198,7 @@
     return kernel_call(
         functools.partial(slope_kernel, scale, rate, step, groups),
         ([((cols, tok), bf16)] if groups > 1 else [((cols // 2, tok), bf16)] * 2)
-        + [((1, tok), f32)]
+        + [((8, tok), f32)]
         + [((cols // groups, chunk), bf16 if groups > 1 else f32)] * groups,
         [key, pre, up, picked, front] + before,
         flops=4 * tok * cols * chunk,
@@ -363,8 +364,10 @@
     kernels = n_t == 2 and sub % 128 == 0 and share <= 128 and chunk % 256 == 0
 
     farthest = sorted(range(1, n_c), reverse=True)
-    sent = [part(second_store, c ^ m, chunk, 0) for m in farthest]
-    act_out = after(act, *sent)
+    sent = [part(second_store, c ^ farthest[0], chunk, 0)]
+    act_out = after(act, sent[0])
+    rest = after(second_store, sent[0])
+    sent += [part(rest, c ^ m, chunk, 0) for m in farthest[1:]]
     weights = {m: swap(piece, "col", m) for m, piece in zip(farthest, sent)}
     mine = after(residual[0, 0], *sent)
     resid_all = [swap(mine, "tp", t) for t in range(n_t)]

time: 240 us -> 242 us (level)
    dynamic_slice x6 -> x7, local copies, waits for them, and re-layouts: 5.15 us -> 6.82 us  [part(): return lax.dynamic_slice_in_dim(values, index * size, size, dim)]
where the time goes in v2:
time: 242 us; the launch traced here: 241 us
  waiting for transfers between devices  110 us (45%)
  starting transfers between devices  56.9 us (24%)
  Pallas kernels  36.7 us (15%)
  local copies, waits for them, and re-layouts  19.3 us (8%)
  matrix products  11.3 us (5%)
  between operations  3.83 us (2%)
  other arithmetic  2.98 us (1%)
    ppermute x41, waiting for transfers between devices, swap(): return lax.ppermute(values, axis, [(i, i ^ step) for i in range(count)])  110 us
    ppermute x41, starting transfers between devices, swap(): return lax.ppermute(values, axis, [(i, i ^ step) for i in range(count)])  56.9 us
    pallas_call x19, Pallas kernels, kernel_call(): pl.pallas_call(kernel, in_specs=[smem if x.size < 16 else vmem for x in a...  26.1 us
    dot_general x5, matrix products, on_device(): jnp.dot(after(a, *behind), first_store, preferred_element_type=f32)  11.3 us
    pallas_call x2, Pallas kernels, lead(): pl.pallas_call(functools.partial(lead_kernel, share), grid=(hid // step,)...  10.6 us
    unnamed x46, local copies, waits for them, and re-layouts  9.93 us
    dynamic_slice x7, local copies, waits for them, and re-layouts, part(): return lax.dynamic_slice_in_dim(values, index * size, size, dim)  6.82 us
  transfers between devices with their start and end apart: 41, of which 16 were waited for; matrix products, arithmetic and copies ran while one was open for 9% of the time, Pallas kernels for 14%

profile of v2, /device:TPU:0, one launch (start us, length us, event | category | flops | bytes accessed | tf_op | source)
XLA Modules:
  0.0 240.9 jit_solution(287044962877085016)
XLA Ops:
  0.6 2.3 dynamic-slice_bitcast_fusion
  2.9 3.1 %constant_dynamic-slice_fusion.4 = (bf16[1024,512]{1,0:T(8,128)(2,1)}, bf16[1024,512]{1,0:T(8,128)(2,1)}) fusion(bf16[4096,512]{1,0:T(8,128)(2,1)} %bitcast.73, s32[]{:T(128)S(6)} %select_n.132, s32[]{:T(128)S(6)} %select_n.131), kind=kLoop, calls=%fused_computation.60 | loop fusion | bytes 4194312 | tf_op jit(solution)/shard_map/dynamic_slice | solution.py:42
  6.5 2.5 %collective-permute-start.2 = (bf16[256,4096]{1,0:T(8,128)(2,1)}, bf16[256,4096]{1,0:T(8,128)(2,1)}, u32[]{:S(2)}, u32[]{:S(2)}) collective-permute-start(bf16[256,4096]{1,0:T(8,128)(2,1)} %bitcast.11.refs_0_), channel_id=1, source_target_pairs={{0,8},{8,0},{16,24},{24,16},{1,9},{9,1},{17,25},{25,17},{2,10},{10... | collective-permute-start | bytes 6291464 | tf_op jit(solution)/shard_map/ppermute | solution.py:25
  12.0 2.6 %collective-permute-start.14 = (bf16[1024,512]{1,0:T(8,128)(2,1)}, bf16[1024,512]{1,0:T(8,128)(2,1)S(1)}, u32[]{:S(2)}, u32[]{:S(2)}) collective-permute-start(bf16[1024,512]{1,0:T(8,128)(2,1)} %get-tuple-element.99), channel_id=1, source_target_pairs={{0,4},{2,6},{4,0},{6,2},{1,5},{3,7},{5,1},{7,3},{8,12},{10,14},{12... | collective-permute-start | bytes 3145736 | tf_op jit(solution)/shard_map/ppermute | solution.py:25
  14.8 4.1 %copy.15 = bf16[1,1,256,4096]{2,3,1,0:T(8,128)(2,1)} copy(bf16[1,1,256,4096]{3,2,1,0:T(8,128)(2,1)} %param.12) | data formatting | bytes 4194304 | tf_op args[2]
  19.7 4.1 %fusion = bf16[256,512]{1,0:T(8,128)(2,1)S(1)} fusion(bf16[256,4096]{1,0:T(8,128)(2,1)} %bitcast.11.refs_0_, bf16[1,4096,512]{2,1,0:T(8,128)(2,1)} %param.16), kind=kOutput, calls=%fused_computation.12 | convolution fusion | flops 1074003968 | bytes 6553600 | tf_op jit(solution)/shard_map/dot_general | solution.py:420
  23.7 5.3 %lead.2.refs_5_ = bf16[64,4096]{1,0:T(8,128)(2,1)} custom-call(bf16[4096,512]{1,0:T(8,128)(2,1)} %bitcast.72), custom_call_target="tpu_custom_call" | custom-call | tf_op jit(solution)/shard_map/lead/pallas_call | solution.py:116
  29.1 5.3 %lead.3.piece = bf16[64,4096]{1,0:T(8,128)(2,1)} custom-call(bf16[4096,512]{1,0:T(8,128)(2,1)} %bitcast.74), custom_call_target="tpu_custom_call" | custom-call | tf_op jit(solution)/shard_map/lead/pallas_call | solution.py:116
  38.5 17.1 %collective-permute-done.2.refs_1_ = bf16[256,4096]{1,0:T(8,128)(2,1)} collective-permute-done((bf16[256,4096]{1,0:T(8,128)(2,1)}, bf16[256,4096]{1,0:T(8,128)(2,1)}, u32[]{:S(2)}, u32[]{:S(2)}) %collective-permute-start.2) | collective-permute-done | bytes 2097184 | tf_op jit(solution)/shard_map/ppermute | solution.py:25
  58.7 2.8 %fusion.1 = bf16[256,512]{1,0:T(8,128)(2,1)S(1)} fusion(bf16[256,4096]{1,0:T(8,128)(2,1)} %collective-permute-done.2.refs_1_, bf16[1,4096,512]{2,1,0:T(8,128)(2,1)S(1)} %copy-done.16), kind=kOutput, calls=%fused_computation.13 | convolution fusion | flops 1074003968 | bytes 6553600 | tf_op jit(solution)/shard_map/dot_general | solution.py:420
  64.8 2.8 %fusion.2 = bf16[256,512]{1,0:T(8,128)(2,1)S(1)} fusion(bf16[256,4096]{1,0:T(8,128)(2,1)} %collective-permute-done.5.refs_2_, bf16[1,4096,512]{2,1,0:T(8,128)(2,1)S(1)} %copy-done.16), kind=kOutput, calls=%fused_computation.14 | convolution fusion | flops 1074003968 | bytes 6553600 | tf_op jit(solution)/shard_map/dot_general | solution.py:420
  67.7 3.7 %collective-permute-start.15 = (bf16[1024,512]{1,0:T(8,128)(2,1)S(1)}, bf16[1024,512]{1,0:T(8,128)(2,1)S(1)}, u32[]{:S(2)}, u32[]{:S(2)}) collective-permute-start(bf16[1024,512]{1,0:T(8,128)(2,1)S(1)} %copy-done.18), channel_id=1, source_target_pairs={{0,6},{2,4},{4,2},{6,0},{1,7},{3,5},{5,3},{7,1},{8,14},{10,12},{12... | collective-permute-start | bytes 3145736 | tf_op jit(solution)/shard_map/ppermute | solution.py:25
  71.4 11.5 %collective-permute-done.8.refs_3_ = bf16[128,4096]{1,0:T(8,128)(2,1)S(1)} collective-permute-done((bf16[128,4096]{1,0:T(8,128)(2,1)S(1)}, bf16[128,4096]{1,0:T(8,128)(2,1)S(1)}, u32[]{:S(2)}, u32[]{:S(2)}) %collective-permute-start.8) | collective-permute-done | bytes 1048608 | tf_op jit(solution)/shard_map/ppermute | solution.py:25
  83.8 4.8 %collective-permute-done.9.refs_4_ = bf16[128,4096]{1,0:T(8,128)(2,1)S(1)} collective-permute-done((bf16[128,4096]{1,0:T(8,128)(2,1)S(1)}, bf16[128,4096]{1,0:T(8,128)(2,1)S(1)}, u32[]{:S(2)}, u32[]{:S(2)}) %collective-permute-start.9) | collective-permute-done | bytes 1048608 | tf_op jit(solution)/shard_map/ppermute | solution.py:25
  94.6 2.2 collective-permute-done.4.refs_5_
  96.9 2.6 %collective-permute-start.11 = (bf16[256,256]{1,0:T(8,128)(2,1)S(1)}, bf16[256,256]{1,0:T(8,128)(2,1)S(1)}, u32[]{:S(2)}, u32[]{:S(2)}) collective-permute-start(bf16[256,256]{1,0:T(8,128)(2,1)S(1)} %add_convert_fusion), channel_id=1, source_target_pairs={{0,24},{8,16},{16,8},{24,0},{1,25},{9,17},{17,9},{25,1},{2,26},{10... | collective-permute-start | bytes 393224 | tf_op jit(solution)/shard_map/ppermute | solution.py:25
  99.6 3.2 %collective-permute-done.11.refs_7_ = bf16[256,256]{1,0:T(8,128)(2,1)S(1)} collective-permute-done((bf16[256,256]{1,0:T(8,128)(2,1)S(1)}, bf16[256,256]{1,0:T(8,128)(2,1)S(1)}, u32[]{:S(2)}, u32[]{:S(2)}) %collective-permute-start.11) | collective-permute-done | bytes 131104 | tf_op jit(solution)/shard_map/ppermute | solution.py:25
  102.9 2.8 %collective-permute-start.22 = (bf16[256,1024]{1,0:T(8,128)(2,1)S(1)}, bf16[256,1024]{1,0:T(8,128)(2,1)}, u32[]{:S(2)}, u32[]{:S(2)}) collective-permute-start(bf16[256,1024]{1,0:T(8,128)(2,1)S(1)} %shard_map.129.same), channel_id=1, source_target_pairs={{0,4},{2,6},{4,0},{6,2},{1,5},{3,7},{5,1},{7,3},{8,12},{10,14},{12... | collective-permute-start | bytes 1572872 | tf_op jit(solution)/shard_map/ppermute | solution.py:25
  108.1 30.9 %collective-permute-done.22.same = bf16[256,1024]{1,0:T(8,128)(2,1)} collective-permute-done((bf16[256,1024]{1,0:T(8,128)(2,1)S(1)}, bf16[256,1024]{1,0:T(8,128)(2,1)}, u32[]{:S(2)}, u32[]{:S(2)}) %collective-permute-start.22) | collective-permute-done | bytes 524320 | tf_op jit(solution)/shard_map/ppermute | solution.py:25
  144.4 21.2 %collective-permute-done.27.same = bf16[256,1024]{1,0:T(8,128)(2,1)} collective-permute-done((bf16[256,1024]{1,0:T(8,128)(2,1)}, bf16[256,1024]{1,0:T(8,128)(2,1)}, u32[]{:S(2)}, u32[]{:S(2)}) %collective-permute-start.27) | collective-permute-done | bytes 524320 | tf_op jit(solution)/shard_map/ppermute | solution.py:25
  165.6 2.5 %collective-permute-start.29 = (bf16[1040,256]{1,0:T(8,128)(2,1)}, bf16[1040,256]{1,0:T(8,128)(2,1)S(1)}, u32[]{:S(2)}, u32[]{:S(2)}) collective-permute-start(bf16[1040,256]{1,0:T(8,128)(2,1)} %get-tuple-element.112), channel_id=1, source_target_pairs={{0,6},{2,4},{4,2},{6,0},{1,7},{3,5},{5,3},{7,1},{8,14},{10,12},{12... | collective-permute-start | bytes 1597448 | tf_op jit(solution)/shard_map/ppermute | solution.py:25
  174.0 2.7 %shard_map.134 = (f32[1024,256]{1,0:T(8,128)S(1)}, bf16[256,256]{1,0:T(8,128)(2,1)S(1)}) custom-call(s32[2]{0:T(128)S(1)} %pad_add_fusion.key, bf16[256,1024]{1,0:T(8,128)(2,1)} %collective-permute-done.17.same, bf16[256,1024]{1,0:T(8,128)(2,1)} %collective-permute-done.18.other, bf16[1024,512]{1,0:T(8,128)(2,1)S(1)} %constant_dynamic-slice_fusion.2.refs_0_, ...), custom_call_target="tpu_custom_call" | custom-call | flops 1073741824 | bytes 6422536 | tf_op jit(solution)/shard_map/pallas_call | solution.py:67
  178.6 2.6 %shard_map.137 = (f32[1024,256]{1,0:T(8,128)S(1)}, bf16[256,256]{1,0:T(8,128)(2,1)S(1)}) custom-call(s32[2]{0:T(128)S(1)} %pad_add_fusion.key, bf16[256,1024]{1,0:T(8,128)(2,1)} %collective-permute-done.22.same, bf16[256,1024]{1,0:T(8,128)(2,1)} %collective-permute-done.23.other, bf16[1024,512]{1,0:T(8,128)(2,1)S(1)} %constant_dynamic-slice_fusion.2.refs_0_, ...), custom_call_target="tpu_custom_call" | custom-call | flops 1073741824 | bytes 6422536 | tf_op jit(solution)/shard_map/pallas_call | solution.py:67
  183.3 2.8 %shard_map.140 = (f32[1024,256]{1,0:T(8,128)S(1)}, bf16[256,256]{1,0:T(8,128)(2,1)S(1)}) custom-call(s32[2]{0:T(128)S(1)} %pad_add_fusion.key, bf16[256,1024]{1,0:T(8,128)(2,1)} %collective-permute-done.27.same, bf16[256,1024]{1,0:T(8,128)(2,1)} %collective-permute-done.28.other, bf16[1024,512]{1,0:T(8,128)(2,1)S(1)} %constant_dynamic-slice_fusion.2.refs_0_, ...), custom_call_target="tpu_custom_call" | custom-call | flops 1073741824 | bytes 6422536 | tf_op jit(solution)/shard_map/pallas_call | solution.py:67
  189.2 11.3 %collective-permute-start.30 = (bf16[256,256]{1,0:T(8,128)(2,1)S(1)}, bf16[256,256]{1,0:T(8,128)(2,1)S(1)}, u32[]{:S(2)}, u32[]{:S(2)}) collective-permute-start(bf16[256,256]{1,0:T(8,128)(2,1)S(1)} %get-tuple-element.84), channel_id=1, source_target_pairs={{0,6},{2,4},{4,2},{6,0},{1,7},{3,5},{5,3},{7,1},{8,14},{10,12},{12... | collective-permute-start | bytes 393224 | tf_op jit(solution)/shard_map/ppermute | solution.py:25
  202.8 2.8 %collective-permute-done.21.refs_1_ = bf16[128,256]{1,0:T(8,128)(2,1)S(1)} collective-permute-done((bf16[128,256]{1,0:T(8,128)(2,1)S(1)}, bf16[128,256]{1,0:T(8,128)(2,1)S(1)}, u32[]{:S(2)}, u32[]{:S(2)}) %collective-permute-start.21) | collective-permute-done | bytes 65568 | tf_op jit(solution)/shard_map/ppermute | solution.py:25
  205.6 4.2 %collective-permute-done.26.refs_2_ = bf16[128,256]{1,0:T(8,128)(2,1)S(1)} collective-permute-done((bf16[128,256]{1,0:T(8,128)(2,1)S(1)}, bf16[128,256]{1,0:T(8,128)(2,1)S(1)}, u32[]{:S(2)}, u32[]{:S(2)}) %collective-permute-start.26) | collective-permute-done | bytes 65568 | tf_op jit(solution)/shard_map/ppermute | solution.py:25
  210.9 3.4 %collective-permute-start.39 = (bf16[64,1024]{1,0:T(8,128)(2,1)S(1)}, bf16[64,1024]{1,0:T(8,128)(2,1)S(1)}, u32[]{:S(2)}, u32[]{:S(2)}) collective-permute-start(bf16[64,1024]{1,0:T(8,128)(2,1)S(1)} %get-tuple-element.94), channel_id=1, source_target_pairs={{0,4},{2,6},{4,0},{6,2},{1,5},{3,7},{5,1},{7,3},{8,12},{10,14},{12... | collective-permute-start | bytes 393224 | tf_op jit(solution)/shard_map/ppermute | solution.py:25
  216.4 2.3 collective-permute-done.32
  219.9 2.7 %collective-permute-done.33 = s32[1]{0:T(128)} collective-permute-done((s32[1]{0:T(128)}, s32[1]{0:T(128)}, u32[]{:S(2)}, u32[]{:S(2)}) %collective-permute-start.33) | collective-permute-done | bytes 36 | tf_op jit(solution)/shard_map/ppermute | solution.py:25
  224.7 2.6 %collective-permute-done.34 = s32[1]{0:T(128)} collective-permute-done((s32[1]{0:T(128)}, s32[1]{0:T(128)}, u32[]{:S(2)}, u32[]{:S(2)}) %collective-permute-start.34) | collective-permute-done | bytes 36 | tf_op jit(solution)/shard_map/ppermute | solution.py:25
  231.6 3.5 %shard_map.144.refs_1_.refs_3_ = bf16[1024,4096]{1,0:T(8,128)(2,1)S(1)} custom-call(bf16[256,4096]{1,0:T(8,128)(2,1)} %bitcast.11.refs_0_, bf16[256,4096]{1,0:T(8,128)(2,1)} %collective-permute-done.2.refs_1_, bf16[256,4096]{1,0:T(8,128)(2,1)} %collective-permute-done.5.refs_2_, bf16[128,4096]{1,0:T(8,128)(2,1)S(1)} %copy-done.4, bf16[128,4096]{1,0:T(8,128)(2,1)S(1)} %copy-done.6), custom_call_target="tpu_custom_call" | custom-call | bytes 16777216 | tf_op jit(solution)/shard_map/pallas_call | solution.py:67
  (147 shorter events, 58.9 us)
Async XLA Ops:
  6.0 13.7 %collective-permute-start = (bf16[256,1024]{1,0:T(8,128)(2,1)S(1)}, bf16[256,1024]{1,0:T(8,128)(2,1)S(1)}, u32[]{:S(2)}, u32[]{:S(2)}) collective-permute-start(bf16[256,1024]{1,0:T(8,128)(2,1)S(1)} %bitcast.77), channel_id=1, source_target_pairs={{0,1},{1,0},{2,3},{3,2},{4,5},{5,4},{6,7},{7,6},{8,9},{9,8},{10,11... | collective-permute-start | bytes 1572872 | tf_op jit(solution)/shard_map/ppermute | solution.py:25
  6.5 49.1 %collective-permute-start.2 = (bf16[256,4096]{1,0:T(8,128)(2,1)}, bf16[256,4096]{1,0:T(8,128)(2,1)}, u32[]{:S(2)}, u32[]{:S(2)}) collective-permute-start(bf16[256,4096]{1,0:T(8,128)(2,1)} %bitcast.11.refs_0_), channel_id=1, source_target_pairs={{0,8},{8,0},{16,24},{24,16},{1,9},{9,1},{17,25},{25,17},{2,10},{10... | collective-permute-start | bytes 6291464 | tf_op jit(solution)/shard_map/ppermute | solution.py:25
  9.0 48.1 %collective-permute-start.5 = (bf16[256,4096]{1,0:T(8,128)(2,1)}, bf16[256,4096]{1,0:T(8,128)(2,1)}, u32[]{:S(2)}, u32[]{:S(2)}) collective-permute-start(bf16[256,4096]{1,0:T(8,128)(2,1)} %bitcast.11.refs_0_), channel_id=1, source_target_pairs={{0,16},{8,24},{16,0},{24,8},{1,17},{9,25},{17,1},{25,9},{2,18},{10... | collective-permute-start | bytes 6291464 | tf_op jit(solution)/shard_map/ppermute | solution.py:25
  10.5 96.8 %collective-permute-start.13 = (bf16[1024,512]{1,0:T(8,128)(2,1)}, bf16[1024,512]{1,0:T(8,128)(2,1)S(1)}, u32[]{:S(2)}, u32[]{:S(2)}) collective-permute-start(bf16[1024,512]{1,0:T(8,128)(2,1)} %get-tuple-element.98), channel_id=1, source_target_pairs={{0,2},{2,0},{4,6},{6,4},{1,3},{3,1},{5,7},{7,5},{8,10},{10,8},{12,... | collective-permute-start | bytes 3145736 | tf_op jit(solution)/shard_map/ppermute | solution.py:25
  12.0 127.0 %collective-permute-start.14 = (bf16[1024,512]{1,0:T(8,128)(2,1)}, bf16[1024,512]{1,0:T(8,128)(2,1)S(1)}, u32[]{:S(2)}, u32[]{:S(2)}) collective-permute-start(bf16[1024,512]{1,0:T(8,128)(2,1)} %get-tuple-element.99), channel_id=1, source_target_pairs={{0,4},{2,6},{4,0},{6,2},{1,5},{3,7},{5,1},{7,3},{8,12},{10,14},{12... | collective-permute-start | bytes 3145736 | tf_op jit(solution)/shard_map/ppermute | solution.py:25
  58.3 24.5 %collective-permute-start.8 = (bf16[128,4096]{1,0:T(8,128)(2,1)S(1)}, bf16[128,4096]{1,0:T(8,128)(2,1)S(1)}, u32[]{:S(2)}, u32[]{:S(2)}) collective-permute-start(bf16[128,4096]{1,0:T(8,128)(2,1)S(1)} %slice.28), channel_id=1, source_target_pairs={{0,8},{8,0},{16,24},{24,16},{1,9},{9,1},{17,25},{25,17},{2,10},{10... | collective-permute-start | bytes 3145736 | tf_op jit(solution)/shard_map/ppermute | solution.py:25
  61.6 6.0 %collective-permute-start.3 = (bf16[256,256]{1,0:T(8,128)(2,1)S(1)}, bf16[256,256]{1,0:T(8,128)(2,1)S(1)}, u32[]{:S(2)}, u32[]{:S(2)}) collective-permute-start(bf16[256,256]{1,0:T(8,128)(2,1)S(1)} %constant_dynamic-slice_fusion.1), channel_id=1, source_target_pairs={{0,1},{1,0},{2,3},{3,2},{4,5},{5,4},{6,7},{7,6},{8,9},{9,8},{10,11... | collective-permute-start | bytes 393224 | tf_op jit(solution)/shard_map/ppermute | solution.py:25
  63.0 25.6 %collective-permute-start.9 = (bf16[128,4096]{1,0:T(8,128)(2,1)S(1)}, bf16[128,4096]{1,0:T(8,128)(2,1)S(1)}, u32[]{:S(2)}, u32[]{:S(2)}) collective-permute-start(bf16[128,4096]{1,0:T(8,128)(2,1)S(1)} %slice.29), channel_id=1, source_target_pairs={{0,16},{8,24},{16,0},{24,8},{1,17},{9,25},{17,1},{25,9},{2,18},{10... | collective-permute-start | bytes 3145736 | tf_op jit(solution)/shard_map/ppermute | solution.py:25
  67.7 73.5 %collective-permute-start.15 = (bf16[1024,512]{1,0:T(8,128)(2,1)S(1)}, bf16[1024,512]{1,0:T(8,128)(2,1)S(1)}, u32[]{:S(2)}, u32[]{:S(2)}) collective-permute-start(bf16[1024,512]{1,0:T(8,128)(2,1)S(1)} %copy-done.18), channel_id=1, source_target_pairs={{0,6},{2,4},{4,2},{6,0},{1,7},{3,5},{5,3},{7,1},{8,14},{10,12},{12... | collective-permute-start | bytes 3145736 | tf_op jit(solution)/shard_map/ppermute | solution.py:25
  82.8 10.2 %collective-permute-start.1 = (bf16[256,256]{1,0:T(8,128)(2,1)S(1)}, bf16[256,256]{1,0:T(8,128)(2,1)S(1)}, u32[]{:S(2)}, u32[]{:S(2)}) collective-permute-start(bf16[256,256]{1,0:T(8,128)(2,1)S(1)} %constant_dynamic-slice_fusion.3), channel_id=1, source_target_pairs={{0,1},{1,0},{2,3},{3,2},{4,5},{5,4},{6,7},{7,6},{8,9},{9,8},{10,11... | collective-permute-start | bytes 393224 | tf_op jit(solution)/shard_map/ppermute | solution.py:25
  93.1 6.5 %collective-permute-start.7 = (bf16[256,256]{1,0:T(8,128)(2,1)S(1)}, bf16[256,256]{1,0:T(8,128)(2,1)S(1)}, u32[]{:S(2)}, u32[]{:S(2)}) collective-permute-start(bf16[256,256]{1,0:T(8,128)(2,1)S(1)} %add_convert_fusion.1), channel_id=1, source_target_pairs={{0,16},{8,24},{16,0},{24,8},{1,17},{9,25},{17,1},{25,9},{2,18},{10... | collective-permute-start | bytes 393224 | tf_op jit(solution)/shard_map/ppermute | solution.py:25
  102.9 36.2 %collective-permute-start.22 = (bf16[256,1024]{1,0:T(8,128)(2,1)S(1)}, bf16[256,1024]{1,0:T(8,128)(2,1)}, u32[]{:S(2)}, u32[]{:S(2)}) collective-permute-start(bf16[256,1024]{1,0:T(8,128)(2,1)S(1)} %shard_map.129.same), channel_id=1, source_target_pairs={{0,4},{2,6},{4,0},{6,2},{1,5},{3,7},{5,1},{7,3},{8,12},{10,14},{12... | collective-permute-start | bytes 1572872 | tf_op jit(solution)/shard_map/ppermute | solution.py:25
  105.7 33.4 %collective-permute-start.17 = (bf16[256,1024]{1,0:T(8,128)(2,1)S(1)}, bf16[256,1024]{1,0:T(8,128)(2,1)}, u32[]{:S(2)}, u32[]{:S(2)}) collective-permute-start(bf16[256,1024]{1,0:T(8,128)(2,1)S(1)} %shard_map.129.same), channel_id=1, source_target_pairs={{0,2},{2,0},{4,6},{6,4},{1,3},{3,1},{5,7},{7,5},{8,10},{10,8},{12,... | collective-permute-start | bytes 1572872 | tf_op jit(solution)/shard_map/ppermute | solution.py:25
  107.3 35.0 %collective-permute-start.12 = (bf16[256,1024]{1,0:T(8,128)(2,1)S(1)}, bf16[256,1024]{1,0:T(8,128)(2,1)S(1)}, u32[]{:S(2)}, u32[]{:S(2)}) collective-permute-start(bf16[256,1024]{1,0:T(8,128)(2,1)S(1)} %shard_map.129.same), channel_id=1, source_target_pairs={{0,1},{1,0},{2,3},{3,2},{4,5},{5,4},{6,7},{7,6},{8,9},{9,8},{10,11... | collective-permute-start | bytes 1572872 | tf_op jit(solution)/shard_map/ppermute | solution.py:25
  139.1 26.5 %collective-permute-start.27 = (bf16[256,1024]{1,0:T(8,128)(2,1)}, bf16[256,1024]{1,0:T(8,128)(2,1)}, u32[]{:S(2)}, u32[]{:S(2)}) collective-permute-start(bf16[256,1024]{1,0:T(8,128)(2,1)} %collective-permute-done.22.same), channel_id=1, source_target_pairs={{0,2},{2,0},{4,6},{6,4},{1,3},{3,1},{5,7},{7,5},{8,10},{10,8},{12,... | collective-permute-start | bytes 1572872 | tf_op jit(solution)/shard_map/ppermute | solution.py:25
  139.1 26.5 %collective-permute-start.18 = (bf16[256,1024]{1,0:T(8,128)(2,1)}, bf16[256,1024]{1,0:T(8,128)(2,1)}, u32[]{:S(2)}, u32[]{:S(2)}) collective-permute-start(bf16[256,1024]{1,0:T(8,128)(2,1)} %collective-permute-done.17.same), channel_id=1, source_target_pairs={{0,1},{1,0},{2,3},{3,2},{4,5},{5,4},{6,7},{7,6},{8,9},{9,8},{10,11... | collective-permute-start | bytes 1572872 | tf_op jit(solution)/shard_map/ppermute | solution.py:25
  139.1 37.6 %collective-permute-start.19 = (bf16[1040,256]{1,0:T(8,128)(2,1)}, bf16[1040,256]{1,0:T(8,128)(2,1)}, u32[]{:S(2)}, u32[]{:S(2)}) collective-permute-start(bf16[1040,256]{1,0:T(8,128)(2,1)} %get-tuple-element.113), channel_id=1, source_target_pairs={{0,2},{2,0},{4,6},{6,4},{1,3},{3,1},{5,7},{7,5},{8,10},{10,8},{12,... | collective-permute-start | bytes 1597448 | tf_op jit(solution)/shard_map/ppermute | solution.py:25
  142.1 36.5 %collective-permute-start.23 = (bf16[256,1024]{1,0:T(8,128)(2,1)}, bf16[256,1024]{1,0:T(8,128)(2,1)}, u32[]{:S(2)}, u32[]{:S(2)}) collective-permute-start(bf16[256,1024]{1,0:T(8,128)(2,1)} %collective-permute-done.22.same), channel_id=1, source_target_pairs={{0,1},{1,0},{2,3},{3,2},{4,5},{5,4},{6,7},{7,6},{8,9},{9,8},{10,11... | collective-permute-start | bytes 1572872 | tf_op jit(solution)/shard_map/ppermute | solution.py:25
  143.1 38.2 %collective-permute-start.24 = (bf16[1040,256]{1,0:T(8,128)(2,1)}, bf16[1040,256]{1,0:T(8,128)(2,1)}, u32[]{:S(2)}, u32[]{:S(2)}) collective-permute-start(bf16[1040,256]{1,0:T(8,128)(2,1)} %get-tuple-element.114), channel_id=1, source_target_pairs={{0,4},{2,6},{4,0},{6,2},{1,5},{3,7},{5,1},{7,3},{8,12},{10,14},{12... | collective-permute-start | bytes 1597448 | tf_op jit(solution)/shard_map/ppermute | solution.py:25
  165.6 17.8 %collective-permute-start.28 = (bf16[256,1024]{1,0:T(8,128)(2,1)}, bf16[256,1024]{1,0:T(8,128)(2,1)}, u32[]{:S(2)}, u32[]{:S(2)}) collective-permute-start(bf16[256,1024]{1,0:T(8,128)(2,1)} %collective-permute-done.27.same), channel_id=1, source_target_pairs={{0,1},{1,0},{2,3},{3,2},{4,5},{5,4},{6,7},{7,6},{8,9},{9,8},{10,11... | collective-permute-start | bytes 1572872 | tf_op jit(solution)/shard_map/ppermute | solution.py:25
  165.6 21.9 %collective-permute-start.29 = (bf16[1040,256]{1,0:T(8,128)(2,1)}, bf16[1040,256]{1,0:T(8,128)(2,1)S(1)}, u32[]{:S(2)}, u32[]{:S(2)}) collective-permute-start(bf16[1040,256]{1,0:T(8,128)(2,1)} %get-tuple-element.112), channel_id=1, source_target_pairs={{0,6},{2,4},{4,2},{6,0},{1,7},{3,5},{5,3},{7,1},{8,14},{10,12},{12... | collective-permute-start | bytes 1597448 | tf_op jit(solution)/shard_map/ppermute | solution.py:25
  178.4 22.1 %collective-permute-start.20 = (bf16[128,256]{1,0:T(8,128)(2,1)S(1)}, bf16[128,256]{1,0:T(8,128)(2,1)S(1)}, u32[]{:S(2)}, u32[]{:S(2)}) collective-permute-start(bf16[128,256]{1,0:T(8,128)(2,1)S(1)} %get-tuple-element.73), channel_id=1, source_target_pairs={{0,1},{1,0},{2,3},{3,2},{4,5},{5,4},{6,7},{7,6},{8,9},{9,8},{10,11... | collective-permute-start | bytes 196616 | tf_op jit(solution)/shard_map/ppermute | solution.py:25
  183.0 18.6 %collective-permute-start.25 = (bf16[128,256]{1,0:T(8,128)(2,1)S(1)}, bf16[128,256]{1,0:T(8,128)(2,1)S(1)}, u32[]{:S(2)}, u32[]{:S(2)}) collective-permute-start(bf16[128,256]{1,0:T(8,128)(2,1)S(1)} %get-tuple-element.79), channel_id=1, source_target_pairs={{0,1},{1,0},{2,3},{3,2},{4,5},{5,4},{6,7},{7,6},{8,9},{9,8},{10,11... | collective-permute-start | bytes 196616 | tf_op jit(solution)/shard_map/ppermute | solution.py:25
  189.2 20.6 %collective-permute-start.30 = (bf16[256,256]{1,0:T(8,128)(2,1)S(1)}, bf16[256,256]{1,0:T(8,128)(2,1)S(1)}, u32[]{:S(2)}, u32[]{:S(2)}) collective-permute-start(bf16[256,256]{1,0:T(8,128)(2,1)S(1)} %get-tuple-element.84), channel_id=1, source_target_pairs={{0,6},{2,4},{4,2},{6,0},{1,7},{3,5},{5,3},{7,1},{8,14},{10,12},{12... | collective-permute-start | bytes 393224 | tf_op jit(solution)/shard_map/ppermute | solution.py:25
  201.7 8.1 %collective-permute-start.26 = (bf16[128,256]{1,0:T(8,128)(2,1)S(1)}, bf16[128,256]{1,0:T(8,128)(2,1)S(1)}, u32[]{:S(2)}, u32[]{:S(2)}) collective-permute-start(bf16[128,256]{1,0:T(8,128)(2,1)S(1)} %shard_map.139), channel_id=1, source_target_pairs={{0,4},{2,6},{4,0},{6,2},{1,5},{3,7},{5,1},{7,3},{8,12},{10,14},{12... | collective-permute-start | bytes 196616 | tf_op jit(solution)/shard_map/ppermute | solution.py:25
  210.4 17.5 %collective-permute-start.31 = (bf16[256,256]{1,0:T(8,128)(2,1)S(1)}, bf16[256,256]{1,0:T(8,128)(2,1)S(1)}, u32[]{:S(2)}, u32[]{:S(2)}) collective-permute-start(bf16[256,256]{1,0:T(8,128)(2,1)S(1)} %shard_map.142.mine), channel_id=1, source_target_pairs={{0,1},{1,0},{2,3},{3,2},{4,5},{5,4},{6,7},{7,6},{8,9},{9,8},{10,11... | collective-permute-start | bytes 393224 | tf_op jit(solution)/shard_map/ppermute | solution.py:25
  210.5 19.6 %collective-permute-start.38 = (bf16[64,1024]{1,0:T(8,128)(2,1)S(1)}, bf16[64,1024]{1,0:T(8,128)(2,1)S(1)}, u32[]{:S(2)}, u32[]{:S(2)}) collective-permute-start(bf16[64,1024]{1,0:T(8,128)(2,1)S(1)} %get-tuple-element.93), channel_id=1, source_target_pairs={{0,2},{2,0},{4,6},{6,4},{1,3},{3,1},{5,7},{7,5},{8,10},{10,8},{12,... | collective-permute-start | bytes 393224 | tf_op jit(solution)/shard_map/ppermute | solution.py:25
  210.9 24.2 %collective-permute-start.39 = (bf16[64,1024]{1,0:T(8,128)(2,1)S(1)}, bf16[64,1024]{1,0:T(8,128)(2,1)S(1)}, u32[]{:S(2)}, u32[]{:S(2)}) collective-permute-start(bf16[64,1024]{1,0:T(8,128)(2,1)S(1)} %get-tuple-element.94), channel_id=1, source_target_pairs={{0,4},{2,6},{4,0},{6,2},{1,5},{3,7},{5,1},{7,3},{8,12},{10,14},{12... | collective-permute-start | bytes 393224 | tf_op jit(solution)/shard_map/ppermute | solution.py:25
  214.3 20.8 %collective-permute-start.40 = (bf16[64,1024]{1,0:T(8,128)(2,1)S(1)}, bf16[64,1024]{1,0:T(8,128)(2,1)S(1)}, u32[]{:S(2)}, u32[]{:S(2)}) collective-permute-start(bf16[64,1024]{1,0:T(8,128)(2,1)S(1)} %get-tuple-element.95), channel_id=1, source_target_pairs={{0,6},{2,4},{4,2},{6,0},{1,7},{3,5},{5,3},{7,1},{8,14},{10,12},{12... | collective-permute-start | bytes 393224 | tf_op jit(solution)/shard_map/ppermute | solution.py:25
  227.9 9.7 %collective-permute-start.35 = (bf16[64,256]{1,0:T(8,128)(2,1)S(1)}, bf16[64,256]{1,0:T(8,128)(2,1)S(1)}, u32[]{:S(2)}, u32[]{:S(2)}) collective-permute-start(bf16[64,256]{1,0:T(8,128)(2,1)S(1)} %get-tuple-element.86), channel_id=1, source_target_pairs={{0,8},{8,0},{16,24},{24,16},{1,9},{9,1},{17,25},{25,17},{2,10},{10... | collective-permute-start | bytes 98312 | tf_op jit(solution)/shard_map/ppermute | solution.py:25
  229.5 8.1 %collective-permute-start.36 = (bf16[64,256]{1,0:T(8,128)(2,1)S(1)}, bf16[64,256]{1,0:T(8,128)(2,1)S(1)}, u32[]{:S(2)}, u32[]{:S(2)}) collective-permute-start(bf16[64,256]{1,0:T(8,128)(2,1)S(1)} %get-tuple-element.87), channel_id=1, source_target_pairs={{0,16},{8,24},{16,0},{24,8},{1,17},{9,25},{17,1},{25,9},{2,18},{10... | collective-permute-start | bytes 98312 | tf_op jit(solution)/shard_map/ppermute | solution.py:25
  230.1 7.6 %collective-permute-start.37 = (bf16[64,256]{1,0:T(8,128)(2,1)S(1)}, bf16[64,256]{1,0:T(8,128)(2,1)S(1)}, u32[]{:S(2)}, u32[]{:S(2)}) collective-permute-start(bf16[64,256]{1,0:T(8,128)(2,1)S(1)} %get-tuple-element.88), channel_id=1, source_target_pairs={{0,24},{8,16},{16,8},{24,0},{1,25},{9,17},{17,9},{25,1},{2,26},{10... | collective-permute-start | bytes 98312 | tf_op jit(solution)/shard_map/ppermute | solution.py:25
  (31 other events, 191.7 us)
